TPU v7x, 32 devices: a whole 2x2x4 slice. The times are simulated.
32 devices in a mesh: dp: 4 (over x, core), expert: 8 (over z, y).
Axes of the slice: x: 2, y: 2, z: 4, core: 2. Of those that a mesh axis runs over, the one named last changes fastest.
Arguments:
- tokens: bfloat16 [320, 4096], P('expert', 'dp'), may hold values from -6 to 6
- expert_ids: int32 [320, 8], P('expert'), may hold values from 0 to 15, all different within a row; in each aligned block of 320 rows (0 to 319, 320 to 639, ...) at most 240 rows name the same one
- routing_weights: bfloat16 [320, 8], P('expert'), may hold values from 0.049804688 to 0.29882812
- gate_weight: bfloat16 [16, 768, 4096], P('expert', None, 'dp'), may hold values from -0.09375 to 0.09375
- up_weight: bfloat16 [16, 768, 4096], P('expert', None, 'dp'), may hold values from -0.09375 to 0.09375
- down_weight: bfloat16 [16, 768, 4096], P('expert', None, 'dp'), may hold values from -0.21875 to 0.21875
- out_grad: bfloat16 [320, 4096], P('expert', 'dp'), may hold values from -1.5 to 1.5
Outputs:
- layer_out: bfloat16 [320, 4096], P('expert', 'dp')
- tokens_grad: bfloat16 [320, 4096], P('expert', 'dp')
- routing_grad: float32 [320, 8], P('expert')
- gate_weight_grad: bfloat16 [16, 768, 4096], P('expert', None, 'dp')
- up_weight_grad: bfloat16 [16, 768, 4096], P('expert', None, 'dp')
- down_weight_grad: bfloat16 [16, 768, 4096], P('expert', None, 'dp')
Inputs may be any that keep to these rules, and one draw needn't show every extreme that they name: `expert_ids`: each row names 8 different experts. No expert is named by more than 240 rows, a bound that some block reaches.
All inputs are finite; a program needn't handle non-finite values.
Results may differ from a plain program's by a relative error of at most 0.02.
Values may be sent and summed in bfloat16 or wider, within the bound.
A program may use at most 128 MiB of HBM per device.

v0:
```python
import functools
import jax
import jax.numpy as jnp
from jax import lax
from jax.experimental import pallas as pl
from jax.experimental.pallas import tpu as pltpu
from jax.sharding import PartitionSpec as P

CAP = 240
F32 = jnp.float32
BF = jnp.bfloat16
VM = pl.BlockSpec(memory_space=pltpu.VMEM)


def factor(n):
    slow = 4 if n % 4 == 0 else n
    return slow, n // slow


def remote(src, dst, send, recv, where):
    return pltpu.make_async_remote_copy(
        src_ref=src, dst_ref=dst, send_sem=send, recv_sem=recv,
        device_id=where, device_id_type=pl.DeviceIdType.MESH,
    )


def greet(axis, n):
    me = lax.axis_index(axis)
    sem = pltpu.get_barrier_semaphore()
    for j in range(1, n):
        pl.semaphore_signal(sem, inc=1, device_id={axis: lax.rem(me + j, n)},
                            device_id_type=pl.DeviceIdType.MESH)
    pl.semaphore_wait(sem, n - 1)


def gather_kernel(n, *refs):
    k = 3
    ins, outs = refs[:k], refs[k:2 * k]
    up_s, up_r, dn_s, dn_r, side_s, side_r = refs[2 * k:]
    slow, fast = factor(n)
    me = lax.axis_index("expert")
    a, b = me // fast, lax.rem(me, fast)
    for i in range(k):
        outs[i][me] = ins[i][...]
    greet("expert", n)

    def hop(i, block, target, s_sem, r_sem, own):
        src = ins[i] if own else outs[i].at[block]
        return remote(src, outs[i].at[block], s_sem, r_sem, {"expert": target})

    def side(i, block, slot, j, own):
        return hop(i, block, a * fast + lax.rem(b + j, fast),
                   side_s.at[i, slot, j], side_r.at[i, slot, j], own)

    def up(i, s):
        return hop(i, (a - s) * fast + b, (a + 1) * fast + b, up_s.at[i, s], up_r.at[i, s], s == 0)

    def down(i, s):
        return hop(i, (a + s) * fast + b, (a - 1) * fast + b, dn_s.at[i, s], dn_r.at[i, s], s == 0)

    order = (2, 0, 1)
    for s in range(slow):
        if s > 0:
            for i in order:
                @pl.when(a - s >= 0)
                def _():
                    up(i, s - 1).wait_recv()

                @pl.when(a + s < slow)
                def _():
                    down(i, s - 1).wait_recv()
        if s < slow - 1:
            for i in order:
                @pl.when((a - s >= 0) & (a + 1 < slow))
                def _():
                    up(i, s).start()

                @pl.when((a + s < slow) & (a >= 1))
                def _():
                    down(i, s).start()
        for i in order:
            for j in range(1, fast):
                if s == 0:
                    side(i, me, 0, j, True).start()
                else:
                    @pl.when(a - s >= 0)
                    def _():
                        side(i, (a - s) * fast + b, s, j, False).start()

                    @pl.when(a + s < slow)
                    def _():
                        side(i, (a + s) * fast + b, slow - 1 + s, j, False).start()
    for i in order:
        for s in range(slow):
            if s < slow - 1:
                @pl.when((a - s >= 0) & (a + 1 < slow))
                def _():
                    up(i, s).wait_send()

                @pl.when((a + s < slow) & (a >= 1))
                def _():
                    down(i, s).wait_send()
            for j in range(1, fast):
                if s == 0:
                    side(i, me, 0, j, True).wait()
                else:
                    @pl.when(a - s >= 0)
                    def _():
                        side(i, (a - s) * fast + b, s, j, False).wait()

                    @pl.when(a + s < slow)
                    def _():
                        side(i, (a + s) * fast + b, slow - 1 + s, j, False).wait()


def gather_all(n, tok, grad, meta):
    ins = (tok, grad, meta)
    slow, fast = factor(n)
    dma = pltpu.SemaphoreType.DMA
    return pl.pallas_call(
        functools.partial(gather_kernel, n),
        out_shape=[jax.ShapeDtypeStruct((n,) + x.shape, x.dtype) for x in ins],
        in_specs=[VM] * 3,
        out_specs=[VM] * 3,
        scratch_shapes=[dma((3, slow))] * 4 + [dma((3, 2 * slow, fast))] * 2,
        compiler_params=pltpu.CompilerParams(collective_id=0, has_side_effects=True,
                                             vmem_limit_bytes=48 << 20),
    )(*ins)


def mix_kernel(n, ch, *refs):
    ins, outs = refs[:3], refs[3:6]
    got1, mine, got2, s1, r1, s2, r2, s3, r3, s4, r4 = refs[6:]
    m = n // 2
    me = lax.axis_index("dp")
    chip, core = me // 2, lax.rem(me, 2)
    greet("dp", n)
    partner = {"dp": chip * 2 + 1 - core}

    def pair(i, j, h):
        c = lax.rem(chip + j, m)
        seg = (c * 2 + 1 - core) * ch + h
        return remote(ins[i].at[seg], got1.at[i, j, h], s1.at[i, j, h], r1.at[i, j, h], partner)

    def cross(i, j, h):
        return remote(mine.at[i, j, h], got2.at[i, j, h], s2.at[i, j, h], r2.at[i, j, h],
                      {"dp": lax.rem(chip + j, m) * 2 + core})

    def spread(i, j, h):
        seg = me * ch + h
        return remote(outs[i].at[seg], outs[i].at[seg], s3.at[i, j, h], r3.at[i, j, h],
                      {"dp": lax.rem(chip + j, m) * 2 + core})

    def share(i, j, h):
        seg = (lax.rem(chip + m - j, m) * 2 + core) * ch + h
        return remote(outs[i].at[seg], outs[i].at[seg], s4.at[i, j, h], r4.at[i, j, h], partner)

    order = list(range(1, m)) + [0]
    for h in range(ch):
        for j in order:
            for i in range(3):
                pair(i, j, h).start()
    for h in range(ch):
        for j in order:
            for i in range(3):
                pair(i, j, h).wait_recv()
                seg = (lax.rem(chip + j, m) * 2 + core) * ch + h
                if j > 0:
                    mine[i, j, h] = (ins[i][seg].astype(F32) + got1[i, j, h].astype(F32)).astype(BF)
                    cross(i, j, h).start()
    for h in range(ch):
        total = []
        for i in range(3):
            v = ins[i][me * ch + h].astype(F32) + got1[i, 0, h].astype(F32)
            for j in range(1, m):
                cross(i, j, h).wait_recv()
                v = v + got2[i, j, h].astype(F32)
            total.append(v)
        gate, up, hg = total
        sig = jax.nn.sigmoid(gate)
        outs[0][me * ch + h] = (gate * sig * up).astype(BF)
        outs[1][me * ch + h] = (hg * up * sig * (1.0 + gate * (1.0 - sig))).astype(BF)
        outs[2][me * ch + h] = (hg * gate * sig).astype(BF)
        for i in range(3):
            for j in range(1, m):
                spread(i, j, h).start()
            share(i, 0, h).start()
    for h in range(ch):
        for j in range(1, m):
            for i in range(3):
                spread(i, j, h).wait_recv()
                share(i, j, h).start()
    for h in range(ch):
        for i in range(3):
            for j in range(m):
                pair(i, j, h).wait_send()
                share(i, j, h).wait()
                if j > 0:
                    cross(i, j, h).wait_send()
                    spread(i, j, h).wait_send()


def mix(n, gate, up, hg):
    rows, width = gate.shape
    ch = 3 if rows % (n * 3 * 8) == 0 else 1
    r = rows // (n * ch)
    ins = [x.reshape(n * ch, r, width) for x in (gate, up, hg)]
    m = n // 2
    dma = pltpu.SemaphoreType.DMA
    outs = pl.pallas_call(
        functools.partial(mix_kernel, n, ch),
        out_shape=[jax.ShapeDtypeStruct((n * ch, r, width), BF)] * 3,
        in_specs=[VM] * 3,
        out_specs=[VM] * 3,
        scratch_shapes=[pltpu.VMEM((3, m, ch, r, width), BF)] * 3 + [dma((3, m, ch))] * 8,
        compiler_params=pltpu.CompilerParams(collective_id=1, has_side_effects=True,
                                             vmem_limit_bytes=48 << 20),
    )(*ins)
    return [x.reshape(rows, width) for x in outs]


def reduce_kernel(n, nd, *refs):
    k = 3
    ins, outs = refs[:k], refs[k:2 * k]
    side_b, acc, up_b, dn_b, dots = refs[2 * k:3 * k], refs[3 * k:4 * k], refs[4 * k:5 * k], refs[5 * k:6 * k], refs[6 * k]
    side_s, side_r, up_s, up_r, dn_s, dn_r, dp_s, dp_r = refs[6 * k + 1:]
    slow, fast = factor(n)
    me = lax.axis_index("expert")
    dp = lax.axis_index("dp")
    a, b = me // fast, lax.rem(me, fast)
    sem = pltpu.get_barrier_semaphore()
    for j in range(1, n):
        pl.semaphore_signal(sem, inc=1, device_id={"expert": lax.rem(me + j, n)},
                            device_id_type=pl.DeviceIdType.MESH)
    for j in range(1, nd):
        pl.semaphore_signal(sem, inc=1, device_id={"dp": lax.rem(dp + j, nd)},
                            device_id_type=pl.DeviceIdType.MESH)
    pl.semaphore_wait(sem, n - 1 + nd - 1)

    def side(i, t, j):
        bb = lax.rem(b + j, fast)
        return remote(ins[i].at[t * fast + bb], side_b[i].at[t, j], side_s.at[i, t, j], side_r.at[i, t, j],
                      {"expert": a * fast + bb})

    def up(i, t):
        return remote(acc[i].at[t], up_b[i].at[t], up_s.at[i, t], up_r.at[i, t], {"expert": (a + 1) * fast + b})

    def down(i, t):
        return remote(acc[i].at[t], dn_b[i].at[t], dn_s.at[i, t], dn_r.at[i, t], {"expert": (a - 1) * fast + b})

    far = [t for d in range(slow) for t in ((slow - 1 - d, d) if slow - 1 - d > d else ((d,) if slow - 1 - d == d else ()))]
    for t in far:
        for i in range(k):
            for j in range(1, fast):
                side(i, t, j).start()
    for t in far:
        for i in range(k):
            v = ins[i][t * fast + b].astype(F32)
            for j in range(1, fast):
                side(i, t, j).wait_recv()
                v = v + side_b[i][t, j].astype(F32)
            acc[i][t] = v.astype(acc[i].dtype)

            @pl.when((t > a) & (a > 0))
            def _():
                up(i, t).wait_recv()
                acc[i][t] = (acc[i][t].astype(F32) + up_b[i][t].astype(F32)).astype(acc[i].dtype)

            @pl.when(t > a)
            def _():
                up(i, t).start()

            @pl.when((t < a) & (a < slow - 1))
            def _():
                down(i, t).wait_recv()
                acc[i][t] = (acc[i][t].astype(F32) + dn_b[i][t].astype(F32)).astype(acc[i].dtype)

            @pl.when(t < a)
            def _():
                down(i, t).start()

    def across(j):
        return remote(dots.at[0], dots.at[j], dp_s.at[j], dp_r.at[j], {"dp": lax.rem(dp + j, nd)})

    for i in (2, 0, 1):
        @pl.when(a > 0)
        def _():
            up(i, a).wait_recv()
            acc[i][a] = (acc[i][a].astype(F32) + up_b[i][a].astype(F32)).astype(acc[i].dtype)

        @pl.when(a < slow - 1)
        def _():
            down(i, a).wait_recv()
            acc[i][a] = (acc[i][a].astype(F32) + dn_b[i][a].astype(F32)).astype(acc[i].dtype)

        if i == 2:
            dots[0] = acc[2][a]
            for j in range(1, nd):
                across(j).start()
        else:
            outs[i][...] = acc[i][a]
    v = dots[0]
    for j in range(1, nd):
        across(j).wait()
        v = v + dots[j]
    outs[2][...] = v
    for t in range(slow):
        for i in range(k):
            for j in range(1, fast):
                side(i, t, j).wait_send()

            @pl.when(t > a)
            def _():
                up(i, t).wait_send()

            @pl.when(t < a)
            def _():
                down(i, t).wait_send()


def reduce_all(n, nd, out_rows, in_rows, dot_rows):
    ins = [x.reshape(n, x.shape[0] // n, x.shape[1]) for x in (out_rows, in_rows, dot_rows)]
    slow, fast = factor(n)
    dma = pltpu.SemaphoreType.DMA
    blocks = [(x.shape[1:], x.dtype) for x in ins]
    return pl.pallas_call(
        functools.partial(reduce_kernel, n, nd),
        out_shape=[jax.ShapeDtypeStruct(s, d) for s, d in blocks],
        in_specs=[VM] * 3,
        out_specs=[VM] * 3,
        scratch_shapes=[pltpu.VMEM((slow, fast) + s, d) for s, d in blocks]
        + [pltpu.VMEM((slow,) + s, d) for s, d in blocks] * 3
        + [pltpu.VMEM((nd,) + blocks[2][0], blocks[2][1])]
        + [dma((3, slow, fast))] * 2 + [dma((3, slow))] * 4 + [dma((nd,))] * 2,
        compiler_params=pltpu.CompilerParams(collective_id=2, has_side_effects=True,
                                             vmem_limit_bytes=48 << 20),
    )(*ins)


def dotted(x, y, dx, dy):
    return lax.dot_general(x, y, (((dx,), (dy,)), ((), ())), preferred_element_type=F32)


def rows_kernel(e, match_ref, weight_ref, tok_ref, grad_ref, one_ref, scaled_ref, rows_ref, grows_ref, sgrad_ref):
    t = tok_ref.shape[0]
    lower = (lax.broadcasted_iota(jnp.int32, (t, t), 0) < lax.broadcasted_iota(jnp.int32, (t, t), 1)).astype(F32)
    match = match_ref[...]
    rank = dotted(match.astype(BF), lower.astype(BF), 1, 0)
    place = jnp.where(match > 0.5, rank, -1.0)
    line = lax.broadcasted_iota(jnp.int32, (CAP, t), 0).astype(F32)
    for i in range(e):
        pick = jnp.abs(line - place[i:i + 1, :]) < 0.5
        one = jnp.where(pick, 1.0, 0.0).astype(BF)
        scaled = jnp.where(pick, weight_ref[i:i + 1, :], 0.0).astype(BF)
        one_ref[i] = one
        scaled_ref[i] = scaled
        rows_ref[i] = dotted(one, tok_ref[...], 1, 0).astype(BF)
        grows_ref[i] = dotted(one, grad_ref[...], 1, 0).astype(BF)
        sgrad_ref[i] = dotted(scaled, grad_ref[...], 1, 0).astype(BF)


def make_rows(match, weight, tok, grad):
    e, t = match.shape
    d = tok.shape[1]
    pad = ((0, 16 - e), (0, 0))
    pick = jax.ShapeDtypeStruct((e, CAP, t), BF)
    wide = jax.ShapeDtypeStruct((e, CAP, d), BF)
    return pl.pallas_call(
        functools.partial(rows_kernel, e), out_shape=[pick, pick, wide, wide, wide],
        in_specs=[VM] * 4, out_specs=[VM] * 5,
        compiler_params=pltpu.CompilerParams(vmem_limit_bytes=48 << 20),
    )(jnp.pad(match.astype(F32), pad), jnp.pad(weight, pad), tok, grad)


def weight_kernel(hid, gd, ud, rows, sgrad, gate_o, up_o, down_o):
    gate_o[0] = dotted(gd[0], rows[0], 0, 0).astype(BF)
    up_o[0] = dotted(ud[0], rows[0], 0, 0).astype(BF)
    down_o[0] = dotted(hid[0], sgrad[0], 0, 0).astype(BF)


def weight_grads(hidden, gd, ud, rows, sgrad):
    e, c, f = hidden.shape
    d = rows.shape[2]
    fb = 256 if f % 256 == 0 else f
    narrow = pl.BlockSpec((1, c, fb), lambda i, j: (i, 0, j))
    whole = pl.BlockSpec((1, c, d), lambda i, j: (i, 0, 0))
    out = pl.BlockSpec((1, fb, d), lambda i, j: (i, j, 0))
    return pl.pallas_call(
        weight_kernel, grid=(e, f // fb), out_shape=[jax.ShapeDtypeStruct((e, f, d), BF)] * 3,
        in_specs=[narrow] * 3 + [whole] * 2, out_specs=[out] * 3,
        compiler_params=pltpu.CompilerParams(vmem_limit_bytes=48 << 20),
    )(hidden, gd, ud, rows, sgrad)


def back_kernel(e, gd, ud, gw, uw, one, out):
    total = None
    for i in range(e):
        terms = (dotted(gd[i], gw[i], 1, 0) + dotted(ud[i], uw[i], 1, 0)).astype(BF)
        part = dotted(one[i], terms, 0, 0)
        total = part if total is None else total + part
    out[...] = total.astype(BF)


def back_rows(gd, ud, gate_weight, up_weight, one):
    e, f, d = gate_weight.shape
    t = one.shape[2]
    db = 256 if d % 256 == 0 else d
    delta = pl.BlockSpec(gd.shape, lambda j: (0, 0, 0))
    w = pl.BlockSpec((e, f, db), lambda j: (0, 0, j))
    return pl.pallas_call(
        functools.partial(back_kernel, e), grid=(d // db,), out_shape=jax.ShapeDtypeStruct((t, d), BF),
        in_specs=[delta, delta, w, w, pl.BlockSpec(one.shape, lambda j: (0, 0, 0))],
        out_specs=pl.BlockSpec((t, db), lambda j: (0, j)),
        compiler_params=pltpu.CompilerParams(vmem_limit_bytes=48 << 20),
    )(gd, ud, gate_weight, up_weight, one)


def body(n, nd, tokens, expert_ids, routing_weights, gate_weight, up_weight, down_weight, out_grad):
    e, f, d = gate_weight.shape
    top = expert_ids.shape[1]
    meta = jnp.concatenate([expert_ids.astype(F32), routing_weights.astype(F32)], axis=1)
    meta = jnp.pad(meta, ((0, 0), (0, 128 - 2 * top)))
    tok, grad, meta = gather_all(n, tokens, out_grad, meta)
    tok, grad = tok.reshape(-1, d), grad.reshape(-1, d)
    meta = meta.reshape(-1, 128)
    t = tok.shape[0]
    first = lax.axis_index("expert") * e
    targets = (first + jnp.arange(e, dtype=jnp.int32)).astype(F32)
    hit = meta[None, :, :top] == targets[:, None, None]
    match = jnp.any(hit, axis=2)
    weight = jnp.sum(jnp.where(hit, meta[None, :, top:2 * top], 0.0), axis=2)
    one, scaled, rows, grows, sgrad = make_rows(match, weight, tok, grad)

    def ein(s, x, y):
        return jnp.einsum(s, x, y, preferred_element_type=F32)

    gate_part = ein("ecd,efd->ecf", rows, gate_weight).astype(BF).reshape(e * CAP, f)
    up_part = ein("ecd,efd->ecf", rows, up_weight).astype(BF).reshape(e * CAP, f)
    hg_part = ein("ecd,efd->ecf", sgrad, down_weight).astype(BF).reshape(e * CAP, f)
    hidden, gd, ud = [x.reshape(e, CAP, f) for x in mix(nd, gate_part, up_part, hg_part)]
    eo = ein("ecf,efd->ecd", hidden, down_weight)
    dots = jnp.sum(grows.astype(F32) * eo, axis=2).astype(BF)
    dot_te = jnp.einsum("ect,ec->et", one, dots, preferred_element_type=F32)
    dot_rows = jnp.sum(jnp.where(hit, dot_te[:, :, None], 0.0), axis=0)
    dot_rows = jnp.pad(dot_rows, ((0, 0), (0, 128 - top)))
    out_rows = jnp.einsum("rt,rd->td", scaled.reshape(e * CAP, t), eo.reshape(e * CAP, d).astype(BF), preferred_element_type=F32).astype(BF)
    in_rows = back_rows(gd, ud, gate_weight, up_weight, one)
    layer_out, tokens_grad, routing_grad = reduce_all(n, nd, out_rows, in_rows, dot_rows)
    gate_grad, up_grad, down_grad = weight_grads(hidden, gd, ud, rows, sgrad)
    return layer_out, tokens_grad, routing_grad[:, :top], gate_grad, up_grad, down_grad


def solution(mesh):
    n, nd = mesh.shape["expert"], mesh.shape["dp"]
    w = P("expert", None, "dp")
    x = P("expert", "dp")
    r = P("expert", None)
    return jax.shard_map(functools.partial(body, n, nd), mesh=mesh, in_specs=(x, r, r, w, w, w, x),
                         out_specs=(x, x, r, w, w, w), check_vma=False)
```

profile of v0, /device:TPU:0, one launch (start us, length us, event | category | flops | bytes accessed | tf_op | source)
XLA Modules:
  0.0 126.1 jit_solution(17176919799683309795)
XLA Ops:
  0.6 0.0 copy-start
  0.7 0.8 convert_element_type.43
  1.5 0.8 convert_element_type.44
  2.3 0.1 copy.20
  2.4 0.9 copy-done.21
  3.3 0.0 copy-start.22
  3.3 0.9 copy-done.22
  4.2 25.7 %shard_map.118 = (bf16[8,40,1024]{2,1,0:T(8,128)(2,1)S(1)}, bf16[8,40,1024]{2,1,0:T(8,128)(2,1)S(1)}, f32[8,40,128]{2,1,0:T(8,128)S(1)}) custom-call(bf16[40,1024]{1,0:T(8,128)(2,1)S(1)} %copy-done.21, bf16[40,1024]{1,0:T(8,128)(2,1)S(1)} %copy-done.22, f32[40,128]{1,0:T(8,128)S(1)} %pad.17.refs_2_), custom_call_target="tpu_custom_call" | custom-call | tf_op jit(solution)/shard_map/pallas_call | solution.py:120
  29.8 0.0 copy-start.15
  29.9 0.8 copy-done.15
  30.7 0.0 copy-start.17
  30.7 0.8 copy-done.17
  31.5 0.1 fusion.6
  31.6 0.1 copy.22
  31.7 0.1 copy.21
  31.8 0.1 fusion.2
  31.9 0.1 compare_reduce_fusion
  32.0 0.0 copy-start.16
  32.1 1.1 copy-done.16
  33.1 1.1 copy-done.18
  34.2 1.9 %shard_map.119 = (bf16[2,240,320]{2,1,0:T(8,128)(2,1)S(1)}, bf16[2,240,320]{2,1,0:T(8,128)(2,1)S(1)}, bf16[2,240,1024]{2,1,0:T(8,128)(2,1)S(1)}, bf16[2,240,1024...) custom-call(f32[16,320]{1,0:T(8,128)S(1)} %pad_convert_fusion.match_ref, f32[16,320]{1,0:T(8,128)S(1)} %pad.20.weight_ref, ...), custom_call_target="tpu_custom_call" | custom-call | tf_op jit(solution)/shard_map/pallas_call | solution.py:368
  36.1 0.0 copy-start.19
  36.1 0.0 copy-start.11
  36.1 0.0 copy-start.9
  36.1 0.0 copy-done
  36.2 1.0 convolution_convert_fusion
  37.2 0.0 copy-done.19
  37.2 0.0 copy-start.1
  37.2 0.0 copy-done.23
  37.2 1.0 convolution_convert_fusion.1
  38.2 0.0 copy-done.11
  38.2 0.0 copy-done.9
  38.2 0.8 copy-done.1
  39.1 1.0 convolution_convert_fusion.2
  40.1 30.1 %shard_map.120 = (bf16[12,40,768]{2,1,0:T(8,128)(2,1)S(1)}, bf16[12,40,768]{2,1,0:T(8,128)(2,1)S(1)}, bf16[12,40,768]{2,1,0:T(8,128)(2,1)S(1)}) custom-call(bf16[12,40,768]{2,1,0:T(8,128)(2,1)S(1)} %bitcast.44, bf16[12,40,768]{2,1,0:T(8,128)(2,1)S(1)} %bitcast.43, bf16[12,40,768]{2,1,0:T(8,128)(2,1)S(1)} %bitcast.42), custom_call_target="tpu_custom_call" | custom-call | tf_op jit(solution)/shard_map/pallas_call | solution.py:210
  70.2 0.0 copy-start.3
  70.2 0.0 copy-start.6
  70.2 0.0 copy-start.13
  70.2 1.9 %multiply_reduce_fusion = (bf16[2,240]{1,0:T(2,128)(2,1)S(1)}, bf16[2,240,1024]{2,1,0:T(8,128)(2,1)}) fusion(bf16[2,240,1024]{2,1,0:T(8,128)(2,1)S(1)} %get-tuple-element.33, bf16[2,240,768]{2,1,0:T(8,128)(2,1)S(1)} %bitcast.40, bf16[2,768,1024]{2,1,0:T(8,128)(2,1)S(1)} %copy-done), kind=kOutput, calls=%fused_computation | convolution fusion | flops 756940288 | bytes 5850048 | tf_op jit(solution)/shard_map/ecf,efd->ecd/dot_general | solution.py:435
  72.1 0.2 fusion.4
  72.3 0.0 copy-done.3
  72.3 0.0 copy-done.6
  72.3 0.0 copy-done.13
  72.3 0.1 fusion.3
  72.4 0.8 copy.29
  73.2 0.9 pad.21.clone
  74.1 0.0 copy-start.2
  74.1 1.9 %copy-done.2 = bf16[2,768,1024]{2,1,0:T(8,128)(2,1)S(1)} copy-done((bf16[2,768,1024]{2,1,0:T(8,128)(2,1)S(1)}, bf16[2,768,1024]{2,1,0:T(8,128)(2,1)}, u32[]{:S(2)}) %copy-start.2) | copy-done | bytes 3145752
  76.0 1.1 copy-done.4
  77.1 1.1 copy-done.7
  78.2 5.2 %shard_map.121 = bf16[320,1024]{1,0:T(8,128)(2,1)S(1)} custom-call(bf16[2,240,768]{2,1,0:T(8,128)(2,1)S(1)} %bitcast.34, bf16[2,240,768]{2,1,0:T(8,128)(2,1)S(1)} %bitcast.36, bf16[2,768,1024]{2,1,0:T(8,128)(2,1)S(1)} %copy-done.2, bf16[2,768,1024]{2,1,0:T(8,128)(2,1)} %uw.1, bf16[2,240,320]{2,1,0:T(8,128)(2,1)S(1)} %get-tuple-element.32.one), custom_call_target="tpu_custom_call" | custom-call | tf_op jit(solution)/shard_map/pallas_call | solution.py:410
  83.5 0.0 copy-done.20
  83.5 0.0 copy-done.24
  83.5 0.5 fusion
  84.0 28.8 %shard_map.122 = (bf16[40,1024]{1,0:T(8,128)(2,1)S(1)}, bf16[40,1024]{1,0:T(8,128)(2,1)S(1)}, f32[40,128]{1,0:T(8,128)S(1)}) custom-call(bf16[8,40,1024]{2,1,0:T(8,128)(2,1)S(1)} %bitcast.39, bf16[8,40,1024]{2,1,0:T(8,128)(2,1)S(1)} %bitcast.38, f32[8,40,128]{2,1,0:T(8,128)S(1)} %bitcast.48), custom_call_target="tpu_custom_call" | custom-call | tf_op jit(solution)/shard_map/pallas_call | solution.py:326
  112.8 0.7 copy.25
  113.5 1.1 copy-done.5
  114.6 1.1 copy-done.8
  115.7 1.2 copy-done.10
  116.9 1.2 copy-done.12
  118.1 1.1 copy-done.14
  119.2 5.5 %shard_map.123 = (bf16[2,768,1024]{2,1,0:T(8,128)(2,1)}, bf16[2,768,1024]{2,1,0:T(8,128)(2,1)}, bf16[2,768,1024]{2,1,0:T(8,128)(2,1)}) custom-call(bf16[2,240,768]{2,1,0:T(8,128)(2,1)S(1)} %bitcast.41, bf16[2,240,768]{2,1,0:T(8,128)(2,1)S(1)} %bitcast.35, bf16[2,240,768]{2,1,0:T(8,128)(2,1)S(1)} %bitcast.37, bf16[2,240,1024]{2,1,0:T(8,128)(2,1)S(1)} %copy-done.10, ...), custom_call_target="tpu_custom_call" | custom-call | tf_op jit(solution)/shard_map/pallas_call | solution.py:388
  124.8 0.6 copy.36
  125.4 0.6 copy.37
  (18 shorter events, 0.1 us)
Async XLA Ops:
  0.6 35.5 %copy-start = (bf16[2,768,1024]{2,1,0:T(8,128)(2,1)S(1)}, bf16[2,768,1024]{2,1,0:T(8,128)(2,1)}, u32[]{:S(2)}) copy-start(bf16[2,768,1024]{2,1,0:T(8,128)(2,1)} %param.12) | copy-start | bytes 9437188
  2.4 0.9 copy-start.21
  3.3 0.9 copy-start.22
  29.8 0.8 copy-start.15
  30.7 0.8 copy-start.17
  32.0 1.1 copy-start.16
  33.1 1.1 copy-start.18
  34.2 3.0 %copy-start.23 = (bf16[2,768,1024]{2,1,0:T(8,128)(2,1)S(1)}, bf16[2,768,1024]{2,1,0:T(8,128)(2,1)}, u32[]{:S(2)}) copy-start(bf16[2,768,1024]{2,1,0:T(8,128)(2,1)} %uw.1) | copy-start | bytes 9437188
  36.1 1.1 copy-start.19
  36.1 2.1 %copy-start.11 = (bf16[2,240,1024]{2,1,0:T(8,128)(2,1)}, bf16[2,240,1024]{2,1,0:T(8,128)(2,1)S(1)}, u32[]{:S(2)}) copy-start(bf16[2,240,1024]{2,1,0:T(8,128)(2,1)S(1)} %get-tuple-element.28.sgrad) | copy-start | bytes 2949124
  36.1 2.1 %copy-start.9 = (bf16[2,240,1024]{2,1,0:T(8,128)(2,1)}, bf16[2,240,1024]{2,1,0:T(8,128)(2,1)S(1)}, u32[]{:S(2)}) copy-start(bf16[2,240,1024]{2,1,0:T(8,128)(2,1)S(1)} %get-tuple-element.27.rows) | copy-start | bytes 2949124
  37.2 1.9 %copy-start.1 = (bf16[2,768,1024]{2,1,0:T(8,128)(2,1)S(1)}, bf16[2,768,1024]{2,1,0:T(8,128)(2,1)}, u32[]{:S(2)}) copy-start(bf16[2,768,1024]{2,1,0:T(8,128)(2,1)} %gw.1) | copy-start | bytes 9437188
  70.2 2.1 %copy-start.3 = (bf16[12,40,768]{2,1,0:T(8,128)(2,1)}, bf16[12,40,768]{2,1,0:T(8,128)(2,1)S(1)}, u32[]{:S(2)}) copy-start(bf16[12,40,768]{2,1,0:T(8,128)(2,1)S(1)} %get-tuple-element.30) | copy-start | bytes 2211844
  70.2 2.1 %copy-start.6 = (bf16[12,40,768]{2,1,0:T(8,128)(2,1)}, bf16[12,40,768]{2,1,0:T(8,128)(2,1)S(1)}, u32[]{:S(2)}) copy-start(bf16[12,40,768]{2,1,0:T(8,128)(2,1)S(1)} %get-tuple-element.31) | copy-start | bytes 2211844
  70.2 2.1 %copy-start.13 = (bf16[12,40,768]{2,1,0:T(8,128)(2,1)}, bf16[12,40,768]{2,1,0:T(8,128)(2,1)S(1)}, u32[]{:S(2)}) copy-start(bf16[12,40,768]{2,1,0:T(8,128)(2,1)S(1)} %get-tuple-element.29) | copy-start | bytes 2211844
  74.1 1.9 %copy-start.2 = (bf16[2,768,1024]{2,1,0:T(8,128)(2,1)S(1)}, bf16[2,768,1024]{2,1,0:T(8,128)(2,1)}, u32[]{:S(2)}) copy-start(bf16[2,768,1024]{2,1,0:T(8,128)(2,1)} %gw.1) | copy-start | bytes 9437188
  76.0 1.1 copy-start.4
  77.1 1.1 copy-start.7
  78.2 5.3 %copy-start.20 = (bf16[2,240,320]{2,1,0:T(8,128)(2,1)S(1)}, bf16[2,240,320]{2,1,0:T(8,128)(2,1)}, u32[]{:S(2)}) copy-start(bf16[2,240,320]{2,1,0:T(8,128)(2,1)} %copy-done.19) | copy-start | bytes 921604
  78.2 5.3 %copy-start.24 = (bf16[2,240,1024]{2,1,0:T(8,128)(2,1)S(1)}, bf16[2,240,1024]{2,1,0:T(8,128)(2,1)}, u32[]{:S(2)}) copy-start(bf16[2,240,1024]{2,1,0:T(8,128)(2,1)} %get-tuple-element.61) | copy-start | bytes 2949124
  113.5 1.1 copy-start.5
  114.6 1.1 copy-start.8
  115.7 1.2 copy-start.10
  116.9 1.2 copy-start.12
  118.1 1.1 copy-start.14
where the time goes:
time: 129 us; the launch traced here: 126 us
  Pallas kernels  97.2 us (75%)
  local copies, waits for them, and re-layouts  20.4 us (16%)
  matrix products  5.61 us (4%)
  other arithmetic  1.92 us (1%)
    pallas_call x1, Pallas kernels, mix(): pl.pallas_call(functools.partial(mix_kernel, n, ch), out_shape=[jax.Shape...  30.1 us
    pallas_call x1, Pallas kernels, reduce_all(): pl.pallas_call(functools.partial(reduce_kernel, n, nd), out_shape=[jax.Sh...  28.8 us
    pallas_call x1, Pallas kernels, gather_all(): pl.pallas_call(functools.partial(gather_kernel, n), out_shape=[jax.ShapeD...  25.7 us
    unnamed x54, local copies, waits for them, and re-layouts  19.1 us
    pallas_call x1, Pallas kernels, weight_grads(): pl.pallas_call(weight_kernel, grid=(e, f // fb), out_shape=[jax.ShapeDtyp...  5.55 us
    pallas_call x1, Pallas kernels, back_rows(): pl.pallas_call(functools.partial(back_kernel, e), grid=(d // db,), out_sh...  5.24 us
    dot_general x4, matrix products, ein(): return jnp.einsum(s, x, y, preferred_element_type=F32)  4.92 us

commit v1 on v0

v1 whole, which is shorter than its diff:
```python
import functools
import jax
import jax.numpy as jnp
from jax import lax
from jax.experimental import pallas as pl
from jax.experimental.pallas import tpu as pltpu
from jax.sharding import PartitionSpec as P

CAP = 240
F32 = jnp.float32
BF = jnp.bfloat16
VM = pl.BlockSpec(memory_space=pltpu.VMEM)
ANY = pl.BlockSpec(memory_space=pl.ANY)
MESH = pl.DeviceIdType.MESH


def up_to(x, k):
    return (x + k - 1) // k * k


def factor(n):
    slow = 4 if n % 4 == 0 else 1
    return slow, n // slow


def flip(a, j):
    bit = 1
    while bit <= j:
        if j & bit:
            a = a + bit - 2 * bit * lax.rem(a // bit, 2)
        bit *= 2
    return a


def remote(src, dst, send, recv, where):
    return pltpu.make_async_remote_copy(
        src_ref=src, dst_ref=dst, send_sem=send, recv_sem=recv,
        device_id=where, device_id_type=MESH,
    )


def dotted(x, y, dx, dy):
    return lax.dot_general(x, y, (((dx,), (dy,)), ((), ())), preferred_element_type=F32)


class Plan:
    def __init__(self, n, nd, tb, top, e, f, d):
        self.n, self.nd, self.tb, self.top, self.e, self.f, self.d = n, nd, tb, top, e, f, d
        self.slow, self.fast = factor(n)
        self.m = nd // 2
        self.h = e // 2
        self.experts = n * e
        self.tbp = up_to(tb, 16)
        self.tl = up_to(n * self.tbp, 128)
        order = list(range(self.slow))
        self.zorder = order[0::2] + order[1::2]
        self.nz = max(1, self.slow // 2)
        self.early = self.zorder[:self.nz]
        self.late = self.zorder[self.nz:]
        self.hb = self.nz * self.fast * self.tbp
        n1 = self.nz * self.fast * tb
        n2 = n * tb - n1
        lo = max(0, CAP - n2) // 16 * 16
        hi = min(CAP, up_to(n1, 16))
        self.hi = hi
        spans = []
        half = up_to(self.hb, 128)
        back = self.hb // 128 * 128
        for s0, s1, l0, l1, needs_late in ((0, lo, 0, half, False), (lo, hi, 0, self.tl, True),
                                           (hi, CAP, back, self.tl, True)):
            if s1 > s0:
                spans.append((s0, s1, l0, l1, needs_late))
        self.spans = spans
        self.lo = lo
        self.half, self.back = half, back

    def place(self, jz, jj):
        return self.zorder.index(jz) * self.fast + jj


def main_kernel(p, tok_h, grad_h, ids, wts, gw_h, uw_h, dw_h,
                layer_o, tgrad_o, rg_o, hid, gd, ud, rows, sgrad,
                gw, uw, dw, tokb, gradb, tokf, gradf, wown, wall, one, scaled, grows,
                psend, precv, mine, got, eb, terms, dmat, osend, isend, dsend,
                orb, irb, drb, oacc, iacc, dacc, ozb, izb, dzb, dots,
                wsem, lsem, ms, mr, zs, zr, ys, yr, ps, pr, xs, xr, hs, hr,
                rys, ryr, rzs, rzr, ds_, dr_):
    n, nd, tb, e, f, d = p.n, p.nd, p.tb, p.e, p.f, p.d
    slow, fast, m, h, tbp = p.slow, p.fast, p.m, p.h, p.tbp
    me = lax.axis_index("expert")
    dp = lax.axis_index("dp")
    a, b = me // fast, lax.rem(me, fast)
    chip, core = dp // 2, lax.rem(dp, 2)
    partner = {"dp": chip * 2 + 1 - core}
    spans = p.spans
    nc = len(spans)

    loads = [pltpu.make_async_copy(x, y, wsem.at[i]) for i, (x, y) in enumerate(((gw_h, gw), (uw_h, uw), (dw_h, dw)))]
    mine_in = [pltpu.make_async_copy(x, y.at[me], lsem.at[i]) for i, (x, y) in enumerate(((tok_h, tokb), (grad_h, gradb)))]
    for c in mine_in + loads:
        c.start()

    which = lax.broadcasted_iota(jnp.int32, (p.experts, tb), 0)
    w = jnp.zeros((p.experts, tb), F32)
    for k in range(p.top):
        w = w + jnp.where(which == ids[k:k + 1, :], wts[k:k + 1, :].astype(F32), 0.0)
    wown[...] = jnp.zeros_like(wown)
    wown[:, 0:tb] = w.astype(BF)
    wall[me] = wown[...]

    sem = pltpu.get_barrier_semaphore()
    for j in range(1, n):
        pl.semaphore_signal(sem, inc=1, device_id={"expert": lax.rem(me + j, n)}, device_id_type=MESH)
    for j in range(1, nd):
        pl.semaphore_signal(sem, inc=1, device_id={"dp": lax.rem(dp + j, nd)}, device_id_type=MESH)
    pl.semaphore_wait(sem, n - 1 + nd - 1)

    blocks, homes = (tokb, gradb), (tok_h, grad_h)

    def source(jz, jj):
        return flip(a, jz) * fast + lax.rem(b - jj + fast, fast)

    def meta(j):
        return remote(wown, wall.at[me], ms.at[j], mr.at[j], {"expert": lax.rem(me + j, n)})

    def zcopy(i, jz):
        return remote(homes[i], blocks[i].at[me], zs.at[i, jz], zr.at[i, jz], {"expert": flip(a, jz) * fast + b})

    def ycopy(i, jz, jj):
        blk = source(jz, 0)
        src = homes[i] if jz == 0 else blocks[i].at[blk]
        return remote(src, blocks[i].at[blk], ys.at[i, jz, jj], yr.at[i, jz, jj],
                      {"expert": a * fast + lax.rem(b + jj, fast)})

    def forward(i, jz):
        if jz:
            zcopy(i, jz).wait_recv()
        for jj in range(1, fast):
            ycopy(i, jz, jj).start()

    def spread(i):
        for jz in p.zorder:
            if jz:
                zcopy(i, jz).start()
        forward(i, 0)

    def settle(i, group, flat):
        for jz in group:
            for jj in range(fast):
                if jj:
                    ycopy(i, jz, jj).wait_recv()
                elif jz == 0:
                    mine_in[i].wait()
                at = p.place(jz, jj) * tbp
                flat[at:at + tb] = blocks[i][source(jz, jj)]

    def late_of(i):
        for jz in p.late:
            forward(i, jz)

    for j in range(1, n):
        meta(j).start()
    spread(0)

    tokf[...] = jnp.zeros_like(tokf)
    gradf[...] = jnp.zeros_like(gradf)
    tl = p.tl
    lower = ((lax.broadcasted_iota(jnp.int32, (tl, tl), 0) < lax.broadcasted_iota(jnp.int32, (tl, tl), 1))
             & ((lax.broadcasted_iota(jnp.int32, (tl, tl), 0) < p.hb)
                == (lax.broadcasted_iota(jnp.int32, (tl, tl), 1) < p.hb)))
    lower = jnp.where(lower, 1.0, 0.0).astype(BF)

    for jz in p.early:
        if jz:
            forward(0, jz)
    for j in range(1, n):
        meta(j).wait_recv()

    sub = lax.broadcasted_iota(jnp.int32, (p.experts, 128), 0)
    row = lax.broadcasted_iota(jnp.int32, (16, 128), 0)
    wl = jnp.zeros((16, tl), F32)
    for jz in p.zorder:
        for jj in range(fast):
            full = wall[source(jz, jj)].astype(F32)
            v = jnp.zeros((16, 128), F32)
            for i in range(e):
                v = jnp.where(row == i, jnp.sum(jnp.where(sub == me * e + i, full, 0.0), axis=0, keepdims=True), v)
            if tl > 128:
                v = jnp.concatenate([v, jnp.zeros((16, tl - 128), F32)], axis=1)
            at = p.place(jz, jj) * tbp
            wl = wl + (pltpu.roll(v, at, 1) if at else v)
    match = wl > 0.0
    rank = dotted(jnp.where(match, 1.0, 0.0).astype(BF), lower, 1, 0)
    lane = lax.broadcasted_iota(jnp.int32, (16, tl), 1)
    at_slot = jnp.where(match, jnp.where(lane < p.hb, rank, CAP - 1.0 - rank), -1.0)
    line = lax.broadcasted_iota(jnp.int32, (CAP, tl), 0).astype(F32)
    for i in range(e):
        pick = jnp.abs(line - at_slot[i:i + 1, :]) < 0.5
        one[i] = jnp.where(pick, 1.0, 0.0).astype(BF)
        scaled[i] = jnp.where(pick, wl[i:i + 1, :], 0.0).astype(BF)

    settle(0, p.early, tokf)

    def take(table, flat, out, c):
        s0, s1, l0, l1, _ = spans[c]
        for i in range(e):
            out[i, s0:s1] = dotted(table[i, s0:s1, l0:l1], flat[l0:l1], 1, 0).astype(BF)

    def product(k, i, c):
        s0, s1 = spans[c][:2]
        left = (rows, rows, sgrad)[k]
        right = (gw, uw, dw)[k]
        return dotted(left[i, s0:s1], right[i], 1, 1)

    def pair(k, c):
        s0, s1 = spans[c][:2]
        return remote(psend.at[k, :, s0:s1], precv.at[k, :, s0:s1], ps.at[k, c], pr.at[k, c], partner)

    def cross(k, c, j):
        s0, s1 = spans[c][:2]
        return remote(mine.at[k, :, s0:s1], got.at[k, j, :, s0:s1], xs.at[k, c, j], xr.at[k, c, j],
                      {"dp": lax.rem(chip + j, m) * 2 + core})

    def theirs(k, c):
        s0, s1 = spans[c][:2]
        for u in range(h):
            psend[k, u, s0:s1] = product(k, (1 - core) * h + u, c).astype(BF)
        pair(k, c).start()

    def ours(k, c):
        s0, s1 = spans[c][:2]
        part = [product(k, core * h + u, c) for u in range(h)]
        pair(k, c).wait_recv()
        for u in range(h):
            mine[k, u, s0:s1] = (part[u] + precv[k, u, s0:s1].astype(F32)).astype(BF)
        for j in range(1, m):
            cross(k, c, j).start()

    def total(k, c, u):
        s0, s1 = spans[c][:2]
        v = mine[k, u, s0:s1].astype(F32)
        for j in range(1, m):
            v = v + got[k, j, u, s0:s1].astype(F32)
        return v

    def share(k, c):
        s0, s1 = spans[c][:2]
        full = (hid, gd, ud)[k]
        view = full.at[pl.ds(core * h, h), s0:s1]
        return remote(view, view, hs.at[k, c], hr.at[k, c], partner)

    def make_hidden(c):
        s0, s1 = spans[c][:2]
        for k in (0, 1):
            for j in range(1, m):
                cross(k, c, j).wait_recv()
        for u in range(h):
            gate, up = total(0, c, u), total(1, c, u)
            hid[core * h + u, s0:s1] = (gate * jax.nn.sigmoid(gate) * up).astype(BF)
        share(0, c).start()

    def make_delta(c):
        s0, s1 = spans[c][:2]
        for j in range(1, m):
            cross(2, c, j).wait_recv()
        for u in range(h):
            gate, up, hg = total(0, c, u), total(1, c, u), total(2, c, u)
            sig = jax.nn.sigmoid(gate)
            gd[core * h + u, s0:s1] = (hg * up * sig * (1.0 + gate * (1.0 - sig))).astype(BF)
            ud[core * h + u, s0:s1] = (hg * gate * sig).astype(BF)
        share(1, c).start()
        share(2, c).start()

    first = [c for c in range(nc) if not spans[c][4]]
    rest = [c for c in range(nc) if spans[c][4]]
    for i in range(2):
        loads[i].wait()
    for c in first:
        take(one, tokf, rows, c)
        theirs(0, c)
        theirs(1, c)
    late_of(0)
    for c in first:
        ours(0, c)
        ours(1, c)
    settle(0, p.late, tokf)
    spread(1)
    for c in rest:
        take(one, tokf, rows, c)
        theirs(0, c)
        theirs(1, c)
        ours(0, c)
        ours(1, c)
    for jz in p.zorder:
        if jz:
            forward(1, jz)
    settle(1, p.zorder, gradf)
    loads[2].wait()
    for c in range(nc):
        take(scaled, gradf, sgrad, c)
        theirs(2, c)
        take(one, gradf, grows, c)
        ours(2, c)

    def back(table, i, s0, s1, l0, l1, x):
        return dotted(table[i, s0:s1, l0:l1], x, 0, 0)

    sends = (osend, isend, dsend)
    rbufs = (orb, irb, drb)
    accs = (oacc, iacc, dacc)
    zbufs = (ozb, izb, dzb)

    def ry(i, jz, jj):
        to = a * fast + lax.rem(b + jj, fast)
        return remote(sends[i].at[flip(a, jz) * fast + lax.rem(b + jj, fast)], rbufs[i].at[jz, jj],
                      rys.at[i, jz, jj], ryr.at[i, jz, jj], {"expert": to})

    def rz(i, jz):
        return remote(accs[i].at[jz], zbufs[i].at[jz], rzs.at[i, jz], rzr.at[i, jz],
                      {"expert": flip(a, jz) * fast + b})

    def reply(jz, jj):
        return flip(a, jz) * fast + lax.rem(b + jj, fast)

    def lanes_of(group):
        if group is p.early:
            return 0, p.half, 0
        return p.back, p.tl, p.hb - p.back

    def put(i, group, value, skip, c0, c1):
        for g, jz in enumerate(group):
            for jj in range(fast):
                at = skip + (g * fast + jj) * tbp
                sends[i][reply(jz, (fast - jj) % fast), :, c0:c1] = value[at:at + tb].astype(BF)

    db = 256 if d % 256 == 0 else d

    def expert_out(cs):
        s0, s1 = spans[cs[0]][0], spans[cs[-1]][1]
        for i in range(e):
            dot = jnp.zeros((s1 - s0, 1), F32)
            for c0 in range(0, d, db):
                v = dotted(hid[i, s0:s1], dw[i, :, c0:c0 + db], 1, 0)
                eb[i, s0:s1, c0:c0 + db] = v.astype(BF)
                dot = dot + jnp.sum(v * grows[i, s0:s1, c0:c0 + db].astype(F32), axis=1, keepdims=True)
            at = lax.broadcasted_iota(jnp.int32, (s1 - s0, dmat.shape[2]), 1) == me * e + i
            dmat[i, s0:s1] = jnp.where(at, dot, 0.0).astype(BF)

    def row_terms(cs):
        s0, s1 = spans[cs[0]][0], spans[cs[-1]][1]
        for i in range(e):
            for c0 in range(0, d, db):
                terms[i, s0:s1, c0:c0 + db] = (dotted(gd[i, s0:s1], gw[i, :, c0:c0 + db], 1, 0)
                                               + dotted(ud[i, s0:s1], uw[i, :, c0:c0 + db], 1, 0)).astype(BF)

    def send_sum(i, table, data, group):
        s0, s1 = (0, p.hi) if group is p.early else (p.lo, CAP)
        l0, l1, skip = lanes_of(group)
        for c0 in range(0, d, db):
            v = sum(back(table, x, s0, s1, l0, l1, data[x, s0:s1, c0:c0 + db]) for x in range(e))
            put(i, group, v, skip, c0, c0 + db)
        for jz in reversed(group):
            for jj in range(1, fast):
                ry(i, jz, jj).start()

    def send_dots(group):
        s0, s1 = (0, p.hi) if group is p.early else (p.lo, CAP)
        l0, l1, skip = lanes_of(group)
        v = sum(dotted(dmat[x, s0:s1], one[x, s0:s1, l0:l1], 0, 0) for x in range(e))
        v = v[:p.experts]
        width = l1 - l0
        for g, jz in enumerate(group):
            for jj in range(fast):
                at = skip + (g * fast + jj) * tbp
                sends[2][reply(jz, (fast - jj) % fast)] = (pltpu.roll(v, (width - at) % width, 1) if at else v)[:, :128].astype(BF)
        for jz in reversed(group):
            for jj in range(1, fast):
                ry(2, jz, jj).start()

    def pass_on(i, group):
        for jz in reversed(group):
            v = sends[i][flip(a, jz) * fast + b].astype(F32)
            for jj in range(1, fast):
                ry(i, jz, jj).wait_recv()
                v = v + rbufs[i][jz, jj].astype(F32)
            accs[i][jz] = v.astype(BF)
            if jz:
                rz(i, jz).start()

    def result(i):
        v = accs[i][0].astype(F32)
        for jz in range(1, slow):
            rz(i, jz).wait_recv()
            v = v + zbufs[i][jz].astype(F32)
        return v

    def share_recv(k, cs):
        for c in cs:
            share(k, c).wait_recv()

    near = [c for c in range(nc) if spans[c][0] < p.hi]
    far = [c for c in range(nc) if spans[c][0] >= p.hi]
    for c in near:
        make_hidden(c)
    share_recv(0, near)
    expert_out(near)
    send_sum(0, scaled, eb, p.early)
    send_dots(p.early)
    for c in far:
        make_hidden(c)
    if far:
        share_recv(0, far)
        expert_out(far)
    if p.late:
        send_sum(0, scaled, eb, p.late)
        send_dots(p.late)
    for c in near:
        make_delta(c)
    for i in (0, 2):
        pass_on(i, p.early)
    for k in (1, 2):
        share_recv(k, near)
    row_terms(near)
    send_sum(1, one, terms, p.early)
    for c in far:
        make_delta(c)
    if p.late:
        for i in (0, 2):
            pass_on(i, p.late)
    if far:
        for k in (1, 2):
            share_recv(k, far)
        row_terms(far)
    if p.late:
        send_sum(1, one, terms, p.late)
    pass_on(1, p.early)

    def across(j):
        return remote(dots.at[0], dots.at[j], ds_.at[j], dr_.at[j], {"dp": lax.rem(dp + j, nd)})

    dots[0] = result(2).astype(BF)
    for j in range(1, nd):
        across(j).start()
    if p.late:
        pass_on(1, p.late)
    layer_o[...] = result(0).astype(BF)
    v = dots[0].astype(F32)
    for j in range(1, nd):
        across(j).wait()
        v = v + dots[j].astype(F32)
    v = v[:, :tb]
    for k in range(p.top):
        rg_o[k:k + 1, :] = jnp.sum(jnp.where(which == ids[k:k + 1, :], v, 0.0), axis=0, keepdims=True)
    tgrad_o[...] = result(1).astype(BF)

    for j in range(1, n):
        meta(j).wait_send()
    for i in range(2):
        for jz in range(slow):
            if jz:
                zcopy(i, jz).wait_send()
            for jj in range(1, fast):
                ycopy(i, jz, jj).wait_send()
    for k in range(3):
        for c in range(nc):
            pair(k, c).wait_send()
            share(k, c).wait_send()
            for j in range(1, m):
                cross(k, c, j).wait_send()
    for i in range(3):
        for jz in range(slow):
            if jz:
                rz(i, jz).wait_send()
            for jj in range(1, fast):
                ry(i, jz, jj).wait_send()


def main_call(n, nd, tok, grad, ids, wts, gw, uw, dw):
    e, f, d = gw.shape
    tb, top = tok.shape[0], ids.shape[0]
    p = Plan(n, nd, tb, top, e, f, d)
    nc = len(p.spans)
    vm, dma = pltpu.VMEM, pltpu.SemaphoreType.DMA
    s = jax.ShapeDtypeStruct
    block, el = (tb, d), up_to(p.experts, 128)
    dot = (p.experts, 128)
    per_half = (p.h, CAP, f)
    return pl.pallas_call(
        functools.partial(main_kernel, p),
        out_shape=[s((tb, d), BF), s((tb, d), BF), s((top, tb), F32)] + [s((e, CAP, f), BF)] * 3 + [s((e, CAP, d), BF)] * 2,
        in_specs=[ANY, ANY, VM, VM, ANY, ANY, ANY],
        out_specs=[VM] * 8,
        scratch_shapes=[vm((e, f, d), BF)] * 3 + [vm((n,) + block, BF)] * 2 + [vm((p.tl, d), BF)] * 2
        + [vm(dot, BF), vm((n,) + dot, BF)] + [vm((e, CAP, p.tl), BF)] * 2 + [vm((e, CAP, d), BF)]
        + [vm((3,) + per_half, BF)] * 3 + [vm((3, p.m) + per_half, BF)]
        + [vm((e, CAP, d), BF)] * 2 + [vm((e, CAP, el), BF)]
        + [vm((n,) + block, BF)] * 2 + [vm((n,) + dot, BF)]
        + [vm((p.slow, p.fast) + block, BF)] * 2 + [vm((p.slow, p.fast) + dot, BF)]
        + ([vm((p.slow,) + block, BF)] * 2 + [vm((p.slow,) + dot, BF)]) * 2
        + [vm((nd,) + dot, BF)]
        + [dma((3,)), dma((2,))] + [dma((n,))] * 2 + [dma((2, p.slow))] * 2 + [dma((2, p.slow, p.fast))] * 2
        + [dma((3, nc))] * 2 + [dma((3, nc, p.m))] * 2 + [dma((3, nc))] * 2
        + [dma((3, p.slow, p.fast))] * 2 + [dma((3, p.slow))] * 2 + [dma((nd,))] * 2,
        compiler_params=pltpu.CompilerParams(collective_id=0, has_side_effects=True, vmem_limit_bytes=54 << 20),
    )(tok, grad, ids, wts, gw, uw, dw)


def weight_kernel(hid, gd, ud, rows, sgrad, layer, tgrad, rg, layer_o, tgrad_o, rg_o, gate_o, up_o, down_o):
    @pl.when((pl.program_id(0) == 0) & (pl.program_id(1) == 0))
    def _():
        layer_o[...] = layer[...]
        tgrad_o[...] = tgrad[...]
        rg_o[...] = rg[...]

    gate_o[0] = dotted(gd[0], rows[0], 0, 0).astype(BF)
    up_o[0] = dotted(ud[0], rows[0], 0, 0).astype(BF)
    down_o[0] = dotted(hid[0], sgrad[0], 0, 0).astype(BF)


def weight_grads(hidden, gd, ud, rows, sgrad, layer, tgrad, rg):
    e, c, f = hidden.shape
    d = rows.shape[2]
    fb = 256 if f % 256 == 0 else f
    narrow = pl.BlockSpec((1, c, fb), lambda i, j: (i, 0, j))
    whole = pl.BlockSpec((1, c, d), lambda i, j: (i, 0, 0))
    out = pl.BlockSpec((1, fb, d), lambda i, j: (i, j, 0))
    small = [pl.BlockSpec(x.shape, lambda i, j: (0, 0)) for x in (layer, tgrad, rg)]
    return pl.pallas_call(
        weight_kernel, grid=(e, f // fb),
        out_shape=[jax.ShapeDtypeStruct(x.shape, x.dtype) for x in (layer, tgrad, rg)]
        + [jax.ShapeDtypeStruct((e, f, d), BF)] * 3,
        in_specs=[narrow] * 3 + [whole] * 2 + small, out_specs=small + [out] * 3,
        compiler_params=pltpu.CompilerParams(vmem_limit_bytes=24 << 20),
    )(hidden, gd, ud, rows, sgrad, layer, tgrad, rg)


def body(n, nd, tokens, expert_ids, routing_weights, gate_weight, up_weight, down_weight, out_grad):
    layer, tgrad, rg, hid, gd, ud, rows, sgrad = main_call(
        n, nd, tokens, out_grad, expert_ids.T, routing_weights.T, gate_weight, up_weight, down_weight)
    layer, tgrad, rg, gate_grad, up_grad, down_grad = weight_grads(hid, gd, ud, rows, sgrad, layer, tgrad, rg)
    return layer, tgrad, rg.T, gate_grad, up_grad, down_grad


def solution(mesh):
    n, nd = mesh.shape["expert"], mesh.shape["dp"]
    w = P("expert", None, "dp")
    x = P("expert", "dp")
    r = P("expert", None)
    return jax.shard_map(functools.partial(body, n, nd), mesh=mesh, in_specs=(x, r, r, w, w, w, x),
                         out_specs=(x, x, r, w, w, w), check_vma=False)
```

time: 129 us -> 88.9 us (0.69); the launches traced: 126 us -> 88.4 us
  Pallas kernels: 97.2 us -> 79.6 us
  local copies, waits for them, and re-layouts: 20.4 us -> 8.19 us
  matrix products: 5.61 us -> 0 us
  other arithmetic: 1.92 us -> 0 us
    pallas_call x5 -> x1, Pallas kernels: 91.7 us -> 74 us  [main_call(): pl.pallas_call(functools.partial(main_kernel, p), out_shape=[s((tb, d), B...]
    unnamed x54 -> x16, local copies, waits for them, and re-layouts: 19.1 us -> 8.19 us
    dot_general x6 -> x0, matrix products: 5.61 us -> none  [the longest x4 4.92 us: ein(): return jnp.einsum(s, x, y, preferred_element_type=F32)]
    convert_element_type x3 -> x0, other arithmetic: 1.62 us -> none  [the longest x1 0.84 us: body(): expert_ids.astype(F32)]
where the time goes in v1:
time: 88.9 us; the launch traced here: 88.4 us
  Pallas kernels  79.6 us (90%)
  local copies, waits for them, and re-layouts  8.19 us (9%)
    pallas_call x1, Pallas kernels, main_call(): pl.pallas_call(functools.partial(main_kernel, p), out_shape=[s((tb, d), B...  74 us
    unnamed x16, local copies, waits for them, and re-layouts  8.19 us
    pallas_call x1, Pallas kernels, weight_grads(): pl.pallas_call(weight_kernel, grid=(e, f // fb), out_shape=[jax.ShapeDtyp...  5.62 us

profile of v1, /device:TPU:0, one launch (start us, length us, event | category | flops | bytes accessed | tf_op | source)
XLA Modules:
  0.0 88.4 jit_solution(2041193358806063172)
XLA Ops:
  0.6 74.0 %shard_map.118 = (bf16[40,1024]{1,0:T(8,128)(2,1)}, bf16[40,1024]{1,0:T(8,128)(2,1)}, f32[8,40]{1,0:T(8,128)}, bf16[2,240,768]{2,1,0:T(8,128)(2,1)}, bf16[2,240,...) custom-call(bf16[40,1024]{1,0:T(8,128)(2,1)} %tok_h.1, ...), custom_call_target="tpu_custom_call" | custom-call | tf_op jit(solution)/shard_map/pallas_call | solution.py:488
  74.6 0.0 copy-start
  74.6 1.2 %copy-done = bf16[2,240,1024]{2,1,0:T(8,128)(2,1)S(1)} copy-done((bf16[2,240,1024]{2,1,0:T(8,128)(2,1)S(1)}, bf16[2,240,1024]{2,1,0:T(8,128)(2,1)}, u32[]{:S(2)}) %copy-start) | copy-done | bytes 983064
  75.8 0.0 copy-start.1
  75.8 1.2 %copy-done.1 = bf16[2,240,1024]{2,1,0:T(8,128)(2,1)S(1)} copy-done((bf16[2,240,1024]{2,1,0:T(8,128)(2,1)S(1)}, bf16[2,240,1024]{2,1,0:T(8,128)(2,1)}, u32[]{:S(2)}) %copy-start.1) | copy-done | bytes 983064
  77.0 0.0 copy-start.2
  77.0 1.1 %copy-done.2 = bf16[2,240,768]{2,1,0:T(8,128)(2,1)S(1)} copy-done((bf16[2,240,768]{2,1,0:T(8,128)(2,1)S(1)}, bf16[2,240,768]{2,1,0:T(8,128)(2,1)}, u32[]{:S(2)}) %copy-start.2) | copy-done | bytes 737304
  78.1 0.0 copy-start.3
  78.1 1.1 %copy-done.3 = bf16[2,240,768]{2,1,0:T(8,128)(2,1)S(1)} copy-done((bf16[2,240,768]{2,1,0:T(8,128)(2,1)S(1)}, bf16[2,240,768]{2,1,0:T(8,128)(2,1)}, u32[]{:S(2)}) %copy-start.3) | copy-done | bytes 737304
  79.3 0.0 copy-start.4
  79.3 1.1 %copy-done.4 = bf16[2,240,768]{2,1,0:T(8,128)(2,1)S(1)} copy-done((bf16[2,240,768]{2,1,0:T(8,128)(2,1)S(1)}, bf16[2,240,768]{2,1,0:T(8,128)(2,1)}, u32[]{:S(2)}) %copy-start.4) | copy-done | bytes 737304
  80.4 0.0 copy-start.5
  80.4 0.9 %copy-done.5 = bf16[40,1024]{1,0:T(8,128)(2,1)S(1)} copy-done((bf16[40,1024]{1,0:T(8,128)(2,1)S(1)}, bf16[40,1024]{1,0:T(8,128)(2,1)}, u32[]{:S(2)}) %copy-start.5) | copy-done | bytes 81944
  81.3 0.0 copy-start.6
  81.3 0.9 %copy-done.6 = bf16[40,1024]{1,0:T(8,128)(2,1)S(1)} copy-done((bf16[40,1024]{1,0:T(8,128)(2,1)S(1)}, bf16[40,1024]{1,0:T(8,128)(2,1)}, u32[]{:S(2)}) %copy-start.6) | copy-done | bytes 81944
  82.1 0.0 copy-start.7
  82.2 0.7 copy-done.7
  82.8 5.6 %shard_map.119 = (bf16[40,1024]{1,0:T(8,128)(2,1)}, bf16[40,1024]{1,0:T(8,128)(2,1)}, f32[8,40]{1,0:T(8,128)}, bf16[2,768,1024]{2,1,0:T(8,128)(2,1)}, bf16[2,768...) custom-call(bf16[2,240,768]{2,1,0:T(8,128)(2,1)S(1)} %copy-done.2, bf16[2,240,768]{2,1,0:T(8,128)(2,1)S(1)} %copy-done.3, ...), custom_call_target="tpu_custom_call" | custom-call | tf_op jit(solution)/shard_map/pallas_call | solution.py:528
Async XLA Ops:
  74.6 1.2 %copy-start = (bf16[2,240,1024]{2,1,0:T(8,128)(2,1)S(1)}, bf16[2,240,1024]{2,1,0:T(8,128)(2,1)}, u32[]{:S(2)}) copy-start(bf16[2,240,1024]{2,1,0:T(8,128)(2,1)} %get-tuple-element.23.rows) | copy-start | bytes 2949124
  75.8 1.2 %copy-start.1 = (bf16[2,240,1024]{2,1,0:T(8,128)(2,1)S(1)}, bf16[2,240,1024]{2,1,0:T(8,128)(2,1)}, u32[]{:S(2)}) copy-start(bf16[2,240,1024]{2,1,0:T(8,128)(2,1)} %get-tuple-element.24.sgrad) | copy-start | bytes 2949124
  77.0 1.1 %copy-start.2 = (bf16[2,240,768]{2,1,0:T(8,128)(2,1)S(1)}, bf16[2,240,768]{2,1,0:T(8,128)(2,1)}, u32[]{:S(2)}) copy-start(bf16[2,240,768]{2,1,0:T(8,128)(2,1)} %get-tuple-element.20.hid) | copy-start | bytes 2211844
  78.1 1.1 %copy-start.3 = (bf16[2,240,768]{2,1,0:T(8,128)(2,1)S(1)}, bf16[2,240,768]{2,1,0:T(8,128)(2,1)}, u32[]{:S(2)}) copy-start(bf16[2,240,768]{2,1,0:T(8,128)(2,1)} %get-tuple-element.21.gd) | copy-start | bytes 2211844
  79.3 1.1 %copy-start.4 = (bf16[2,240,768]{2,1,0:T(8,128)(2,1)S(1)}, bf16[2,240,768]{2,1,0:T(8,128)(2,1)}, u32[]{:S(2)}) copy-start(bf16[2,240,768]{2,1,0:T(8,128)(2,1)} %get-tuple-element.22.ud) | copy-start | bytes 2211844
  80.4 0.9 %copy-start.5 = (bf16[40,1024]{1,0:T(8,128)(2,1)S(1)}, bf16[40,1024]{1,0:T(8,128)(2,1)}, u32[]{:S(2)}) copy-start(bf16[40,1024]{1,0:T(8,128)(2,1)} %get-tuple-element.25.layer) | copy-start | bytes 245764
  81.3 0.9 %copy-start.6 = (bf16[40,1024]{1,0:T(8,128)(2,1)S(1)}, bf16[40,1024]{1,0:T(8,128)(2,1)}, u32[]{:S(2)}) copy-start(bf16[40,1024]{1,0:T(8,128)(2,1)} %get-tuple-element.26.tgrad) | copy-start | bytes 245764
  82.1 0.7 copy-start.7

commit v2 on v1

--- a/solution.py
+++ b/solution.py
@@ -11,6 +11,7 @@
 BF = jnp.bfloat16
 VM = pl.BlockSpec(memory_space=pltpu.VMEM)
 ANY = pl.BlockSpec(memory_space=pl.ANY)
+HBM = pl.BlockSpec(memory_space=pltpu.HBM)
 MESH = pl.DeviceIdType.MESH
 
 
@@ -78,9 +79,9 @@
         return self.zorder.index(jz) * self.fast + jj
 
 
-def main_kernel(p, tok_h, grad_h, ids, wts, gw_h, uw_h, dw_h,
-                layer_o, tgrad_o, rg_o, hid, gd, ud, rows, sgrad,
-                gw, uw, dw, tokb, gradb, tokf, gradf, wown, wall, one, scaled, grows,
+def main_kernel(p, tok_h, grad_h, ids_h, wts_h, gw_h, uw_h, dw_h,
+                layer_o, tgrad_o, rg_o, gate_o, up_o, down_o,
+                ids, wts, hid, gd, ud, rows, sgrad, gw, uw, dw, tokb, gradb, tokf, gradf, wown, wall, one, scaled, grows,
                 psend, precv, mine, got, eb, terms, dmat, osend, isend, dsend,
                 orb, irb, drb, oacc, iacc, dacc, ozb, izb, dzb, dots,
                 wsem, lsem, ms, mr, zs, zr, ys, yr, ps, pr, xs, xr, hs, hr,
@@ -97,8 +98,11 @@
 
     loads = [pltpu.make_async_copy(x, y, wsem.at[i]) for i, (x, y) in enumerate(((gw_h, gw), (uw_h, uw), (dw_h, dw)))]
     mine_in = [pltpu.make_async_copy(x, y.at[me], lsem.at[i]) for i, (x, y) in enumerate(((tok_h, tokb), (grad_h, gradb)))]
-    for c in mine_in + loads:
+    routing = [pltpu.make_async_copy(x, y, lsem.at[2 + i]) for i, (x, y) in enumerate(((ids_h, ids), (wts_h, wts)))]
+    for c in routing + mine_in + loads:
         c.start()
+    for c in routing:
+        c.wait()
 
     which = lax.broadcasted_iota(jnp.int32, (p.experts, tb), 0)
     w = jnp.zeros((p.experts, tb), F32)
@@ -137,12 +141,6 @@
             zcopy(i, jz).wait_recv()
         for jj in range(1, fast):
             ycopy(i, jz, jj).start()
-
-    def spread(i):
-        for jz in p.zorder:
-            if jz:
-                zcopy(i, jz).start()
-        forward(i, 0)
 
     def settle(i, group, flat):
         for jz in group:
@@ -154,13 +152,15 @@
                 at = p.place(jz, jj) * tbp
                 flat[at:at + tb] = blocks[i][source(jz, jj)]
 
-    def late_of(i):
-        for jz in p.late:
-            forward(i, jz)
-
     for j in range(1, n):
         meta(j).start()
-    spread(0)
+    head = p.early + p.late[:1]
+    tail = p.late[1:]
+    for jz in head:
+        if jz:
+            zcopy(0, jz).start()
+    forward(0, 0)
+    forward(1, 0)
 
     tokf[...] = jnp.zeros_like(tokf)
     gradf[...] = jnp.zeros_like(gradf)
@@ -173,6 +173,11 @@
     for jz in p.early:
         if jz:
             forward(0, jz)
+    for jz in tail:
+        zcopy(0, jz).start()
+    for jz in p.late[:1]:
+        zcopy(1, jz).start()
+        forward(0, jz)
     for j in range(1, n):
         meta(j).wait_recv()
 
@@ -201,40 +206,46 @@
 
     settle(0, p.early, tokf)
 
-    def take(table, flat, out, c):
-        s0, s1, l0, l1, _ = spans[c]
-        for i in range(e):
-            out[i, s0:s1] = dotted(table[i, s0:s1, l0:l1], flat[l0:l1], 1, 0).astype(BF)
-
-    def product(k, i, c):
-        s0, s1 = spans[c][:2]
+    def reach(cs):
+        return spans[cs[0]][0], spans[cs[-1]][1]
+
+    def take(table, flat, out, cs):
+        for c in cs:
+            s0, s1, l0, l1, _ = spans[c]
+            for i in range(e):
+                out[i, s0:s1] = dotted(table[i, s0:s1, l0:l1], flat[l0:l1], 1, 0).astype(BF)
+
+    def product(k, i, cs):
+        s0, s1 = reach(cs)
         left = (rows, rows, sgrad)[k]
         right = (gw, uw, dw)[k]
         return dotted(left[i, s0:s1], right[i], 1, 1)
 
-    def pair(k, c):
-        s0, s1 = spans[c][:2]
-        return remote(psend.at[k, :, s0:s1], precv.at[k, :, s0:s1], ps.at[k, c], pr.at[k, c], partner)
+    def pair(k, cs):
+        s0, s1 = reach(cs)
+        return remote(psend.at[k, :, s0:s1], precv.at[k, :, s0:s1], ps.at[k, cs[0]], pr.at[k, cs[0]], partner)
 
     def cross(k, c, j):
         s0, s1 = spans[c][:2]
         return remote(mine.at[k, :, s0:s1], got.at[k, j, :, s0:s1], xs.at[k, c, j], xr.at[k, c, j],
                       {"dp": lax.rem(chip + j, m) * 2 + core})
 
-    def theirs(k, c):
-        s0, s1 = spans[c][:2]
+    def theirs(k, cs):
+        s0, s1 = reach(cs)
         for u in range(h):
-            psend[k, u, s0:s1] = product(k, (1 - core) * h + u, c).astype(BF)
-        pair(k, c).start()
-
-    def ours(k, c):
-        s0, s1 = spans[c][:2]
-        part = [product(k, core * h + u, c) for u in range(h)]
-        pair(k, c).wait_recv()
-        for u in range(h):
-            mine[k, u, s0:s1] = (part[u] + precv[k, u, s0:s1].astype(F32)).astype(BF)
-        for j in range(1, m):
-            cross(k, c, j).start()
+            psend[k, u, s0:s1] = product(k, (1 - core) * h + u, cs).astype(BF)
+        pair(k, cs).start()
+
+    def ours(k, cs):
+        g0 = spans[cs[0]][0]
+        part = [product(k, core * h + u, cs) for u in range(h)]
+        pair(k, cs).wait_recv()
+        for c in cs:
+            s0, s1 = spans[c][:2]
+            for u in range(h):
+                mine[k, u, s0:s1] = (part[u][s0 - g0:s1 - g0] + precv[k, u, s0:s1].astype(F32)).astype(BF)
+            for j in range(1, m):
+                cross(k, c, j).start()
 
     def total(k, c, u):
         s0, s1 = spans[c][:2]
@@ -271,37 +282,6 @@
         share(1, c).start()
         share(2, c).start()
 
-    first = [c for c in range(nc) if not spans[c][4]]
-    rest = [c for c in range(nc) if spans[c][4]]
-    for i in range(2):
-        loads[i].wait()
-    for c in first:
-        take(one, tokf, rows, c)
-        theirs(0, c)
-        theirs(1, c)
-    late_of(0)
-    for c in first:
-        ours(0, c)
-        ours(1, c)
-    settle(0, p.late, tokf)
-    spread(1)
-    for c in rest:
-        take(one, tokf, rows, c)
-        theirs(0, c)
-        theirs(1, c)
-        ours(0, c)
-        ours(1, c)
-    for jz in p.zorder:
-        if jz:
-            forward(1, jz)
-    settle(1, p.zorder, gradf)
-    loads[2].wait()
-    for c in range(nc):
-        take(scaled, gradf, sgrad, c)
-        theirs(2, c)
-        take(one, gradf, grows, c)
-        ours(2, c)
-
     def back(table, i, s0, s1, l0, l1, x):
         return dotted(table[i, s0:s1, l0:l1], x, 0, 0)
 
@@ -334,9 +314,10 @@
                 sends[i][reply(jz, (fast - jj) % fast), :, c0:c1] = value[at:at + tb].astype(BF)
 
     db = 256 if d % 256 == 0 else d
+    fb = 256 if f % 256 == 0 else f
 
     def expert_out(cs):
-        s0, s1 = spans[cs[0]][0], spans[cs[-1]][1]
+        s0, s1 = reach(cs)
         for i in range(e):
             dot = jnp.zeros((s1 - s0, 1), F32)
             for c0 in range(0, d, db):
@@ -347,7 +328,7 @@
             dmat[i, s0:s1] = jnp.where(at, dot, 0.0).astype(BF)
 
     def row_terms(cs):
-        s0, s1 = spans[cs[0]][0], spans[cs[-1]][1]
+        s0, s1 = reach(cs)
         for i in range(e):
             for c0 in range(0, d, db):
                 terms[i, s0:s1, c0:c0 + db] = (dotted(gd[i, s0:s1], gw[i, :, c0:c0 + db], 1, 0)
@@ -398,10 +379,57 @@
         for c in cs:
             share(k, c).wait_recv()
 
-    near = [c for c in range(nc) if spans[c][0] < p.hi]
-    far = [c for c in range(nc) if spans[c][0] >= p.hi]
+    def weight_grad(out, left, right, i):
+        for c0 in range(0, f, fb):
+            out[i, c0:c0 + fb] = dotted(left[i, :, c0:c0 + fb], right[i], 0, 0).astype(BF)
+
+    first = [c for c in range(nc) if not spans[c][4]]
+    rest = [c for c in range(nc) if spans[c][4]]
+    every = list(range(nc))
+    near = [c for c in every if spans[c][0] < p.hi]
+    far = [c for c in every if spans[c][0] >= p.hi]
+    done = [c for c in first if c in near]
+
+    loads[0].wait()
+    if first:
+        take(one, tokf, rows, first)
+        theirs(0, first)
+        ours(0, first)
+    for jz in tail:
+        forward(0, jz)
+    for jz in p.zorder:
+        if jz and jz not in p.late[:1]:
+            zcopy(1, jz).start()
+    for jz in p.late[:1]:
+        forward(1, jz)
+    loads[1].wait()
+    if first:
+        theirs(1, first)
+        ours(1, first)
+    settle(0, p.late, tokf)
+    if rest:
+        take(one, tokf, rows, rest)
+        theirs(0, rest)
+        ours(0, rest)
+    for jz in p.early:
+        if jz:
+            forward(1, jz)
+    if rest:
+        theirs(1, rest)
+        ours(1, rest)
+    for jz in tail:
+        forward(1, jz)
+    for c in done:
+        make_hidden(c)
+    loads[2].wait()
+    settle(1, p.zorder, gradf)
+    take(scaled, gradf, sgrad, every)
+    theirs(2, every)
+    take(one, gradf, grows, every)
+    ours(2, every)
     for c in near:
-        make_hidden(c)
+        if c not in done:
+            make_hidden(c)
     share_recv(0, near)
     expert_out(near)
     send_sum(0, scaled, eb, p.early)
@@ -424,15 +452,16 @@
     send_sum(1, one, terms, p.early)
     for c in far:
         make_delta(c)
-    if p.late:
-        for i in (0, 2):
-            pass_on(i, p.late)
     if far:
         for k in (1, 2):
             share_recv(k, far)
         row_terms(far)
     if p.late:
         send_sum(1, one, terms, p.late)
+        for i in (0, 2):
+            pass_on(i, p.late)
+    for i in range(e):
+        weight_grad(gate_o, gd, rows, i)
     pass_on(1, p.early)
 
     def across(j):
@@ -441,8 +470,12 @@
     dots[0] = result(2).astype(BF)
     for j in range(1, nd):
         across(j).start()
+    for i in range(e):
+        weight_grad(up_o, ud, rows, i)
     if p.late:
         pass_on(1, p.late)
+    for i in range(e):
+        weight_grad(down_o, hid, sgrad, i)
     layer_o[...] = result(0).astype(BF)
     v = dots[0].astype(F32)
     for j in range(1, nd):
@@ -463,10 +496,14 @@
                 ycopy(i, jz, jj).wait_send()
     for k in range(3):
         for c in range(nc):
-            pair(k, c).wait_send()
             share(k, c).wait_send()
             for j in range(1, m):
                 cross(k, c, j).wait_send()
+    for k in (0, 1):
+        for cs in (first, rest):
+            if cs:
+                pair(k, cs).wait_send()
+    pair(2, every).wait_send()
     for i in range(3):
         for jz in range(slow):
             if jz:
@@ -481,16 +518,15 @@
     p = Plan(n, nd, tb, top, e, f, d)
     nc = len(p.spans)
     vm, dma = pltpu.VMEM, pltpu.SemaphoreType.DMA
-    s = jax.ShapeDtypeStruct
     block, el = (tb, d), up_to(p.experts, 128)
     dot = (p.experts, 128)
     per_half = (p.h, CAP, f)
     return pl.pallas_call(
         functools.partial(main_kernel, p),
-        out_shape=[s((tb, d), BF), s((tb, d), BF), s((top, tb), F32)] + [s((e, CAP, f), BF)] * 3 + [s((e, CAP, d), BF)] * 2,
-        in_specs=[ANY, ANY, VM, VM, ANY, ANY, ANY],
-        out_specs=[VM] * 8,
-        scratch_shapes=[vm((e, f, d), BF)] * 3 + [vm((n,) + block, BF)] * 2 + [vm((p.tl, d), BF)] * 2
+        out_shape=[vm((tb, d), BF), vm((tb, d), BF), vm((top, tb), F32)] + [vm((e, f, d), BF)] * 3,
+        in_specs=[HBM] * 7,
+        out_specs=[VM] * 6,
+        scratch_shapes=[vm((top, tb), jnp.int32), vm((top, tb), BF)] + [vm((e, CAP, f), BF)] * 3 + [vm((e, CAP, d), BF)] * 2 + [vm((e, f, d), BF)] * 3 + [vm((n,) + block, BF)] * 2 + [vm((p.tl, d), BF)] * 2
         + [vm(dot, BF), vm((n,) + dot, BF)] + [vm((e, CAP, p.tl), BF)] * 2 + [vm((e, CAP, d), BF)]
         + [vm((3,) + per_half, BF)] * 3 + [vm((3, p.m) + per_half, BF)]
         + [vm((e, CAP, d), BF)] * 2 + [vm((e, CAP, el), BF)]
@@ -498,46 +534,36 @@
         + [vm((p.slow, p.fast) + block, BF)] * 2 + [vm((p.slow, p.fast) + dot, BF)]
         + ([vm((p.slow,) + block, BF)] * 2 + [vm((p.slow,) + dot, BF)]) * 2
         + [vm((nd,) + dot, BF)]
-        + [dma((3,)), dma((2,))] + [dma((n,))] * 2 + [dma((2, p.slow))] * 2 + [dma((2, p.slow, p.fast))] * 2
+        + [dma((3,)), dma((4,))] + [dma((n,))] * 2 + [dma((2, p.slow))] * 2 + [dma((2, p.slow, p.fast))] * 2
         + [dma((3, nc))] * 2 + [dma((3, nc, p.m))] * 2 + [dma((3, nc))] * 2
         + [dma((3, p.slow, p.fast))] * 2 + [dma((3, p.slow))] * 2 + [dma((nd,))] * 2,
-        compiler_params=pltpu.CompilerParams(collective_id=0, has_side_effects=True, vmem_limit_bytes=54 << 20),
-    )(tok, grad, ids, wts, gw, uw, dw)
-
-
-def weight_kernel(hid, gd, ud, rows, sgrad, layer, tgrad, rg, layer_o, tgrad_o, rg_o, gate_o, up_o, down_o):
-    @pl.when((pl.program_id(0) == 0) & (pl.program_id(1) == 0))
-    def _():
-        layer_o[...] = layer[...]
-        tgrad_o[...] = tgrad[...]
-        rg_o[...] = rg[...]
-
-    gate_o[0] = dotted(gd[0], rows[0], 0, 0).astype(BF)
-    up_o[0] = dotted(ud[0], rows[0], 0, 0).astype(BF)
-    down_o[0] = dotted(hid[0], sgrad[0], 0, 0).astype(BF)
-
-
-def weight_grads(hidden, gd, ud, rows, sgrad, layer, tgrad, rg):
-    e, c, f = hidden.shape
-    d = rows.shape[2]
-    fb = 256 if f % 256 == 0 else f
-    narrow = pl.BlockSpec((1, c, fb), lambda i, j: (i, 0, j))
-    whole = pl.BlockSpec((1, c, d), lambda i, j: (i, 0, 0))
-    out = pl.BlockSpec((1, fb, d), lambda i, j: (i, j, 0))
-    small = [pl.BlockSpec(x.shape, lambda i, j: (0, 0)) for x in (layer, tgrad, rg)]
+        compiler_params=pltpu.CompilerParams(collective_id=0, has_side_effects=True, vmem_limit_bytes=44 << 20),
+    )(*[pltpu.with_memory_space_constraint(x, pltpu.HBM) for x in (tok, grad, ids, wts, gw, uw, dw)])
+
+
+def flush_kernel(k, *refs):
+    ins, outs, sem = refs[:k], refs[k:2 * k], refs[2 * k]
+    copies = [pltpu.make_async_copy(x, y, sem.at[i]) for i, (x, y) in enumerate(zip(ins, outs))]
+    for c in copies:
+        c.start()
+    for c in copies:
+        c.wait()
+
+
+def flush(*arrays):
+    k = len(arrays)
     return pl.pallas_call(
-        weight_kernel, grid=(e, f // fb),
-        out_shape=[jax.ShapeDtypeStruct(x.shape, x.dtype) for x in (layer, tgrad, rg)]
-        + [jax.ShapeDtypeStruct((e, f, d), BF)] * 3,
-        in_specs=[narrow] * 3 + [whole] * 2 + small, out_specs=small + [out] * 3,
-        compiler_params=pltpu.CompilerParams(vmem_limit_bytes=24 << 20),
-    )(hidden, gd, ud, rows, sgrad, layer, tgrad, rg)
+        functools.partial(flush_kernel, k),
+        out_shape=[jax.ShapeDtypeStruct(x.shape, x.dtype) for x in arrays],
+        in_specs=[VM] * k, out_specs=[ANY] * k,
+        scratch_shapes=[pltpu.SemaphoreType.DMA((k,))],
+        compiler_params=pltpu.CompilerParams(vmem_limit_bytes=4 << 20),
+    )(*[pltpu.with_memory_space_constraint(x, pltpu.VMEM) for x in arrays])
 
 
 def body(n, nd, tokens, expert_ids, routing_weights, gate_weight, up_weight, down_weight, out_grad):
-    layer, tgrad, rg, hid, gd, ud, rows, sgrad = main_call(
-        n, nd, tokens, out_grad, expert_ids.T, routing_weights.T, gate_weight, up_weight, down_weight)
-    layer, tgrad, rg, gate_grad, up_grad, down_grad = weight_grads(hid, gd, ud, rows, sgrad, layer, tgrad, rg)
+    layer, tgrad, rg, gate_grad, up_grad, down_grad = flush(*main_call(
+        n, nd, tokens, out_grad, expert_ids.T, routing_weights.T, gate_weight, up_weight, down_weight))
     return layer, tgrad, rg.T, gate_grad, up_grad, down_grad
 
 

time: 88.9 us -> 68.6 us (0.77)
  Pallas kernels: 79.6 us -> 67.6 us
  local copies, waits for them, and re-layouts: 8.19 us -> 0 us
    pallas_call x2, Pallas kernels: 79.6 us -> 67.6 us  [the longest x1 63.7 us: main_call(): pl.pallas_call(functools.partial(main_kernel, p), out_shape=[vm((tb, d),...]
    unnamed x16 -> x0, local copies, waits for them, and re-layouts: 8.19 us -> none
where the time goes in v2:
time: 68.6 us; the launch traced here: 68.4 us
  Pallas kernels  67.6 us (99%)
  between operations  0.8 us (1%)
    pallas_call x1, Pallas kernels, main_call(): pl.pallas_call(functools.partial(main_kernel, p), out_shape=[vm((tb, d),...  63.7 us
    pallas_call x1, Pallas kernels, flush(): pl.pallas_call(functools.partial(flush_kernel, k), out_shape=[jax.ShapeDt...  3.85 us

profile of v2, /device:TPU:0, one launch (start us, length us, event | category | flops | bytes accessed | tf_op | source)
XLA Modules:
  0.0 68.4 jit_solution(5256622779657154052)
XLA Ops:
  0.6 63.7 %shard_map.118 = (bf16[40,1024]{1,0:T(8,128)(2,1)S(1)}, bf16[40,1024]{1,0:T(8,128)(2,1)S(1)}, f32[8,40]{1,0:T(8,128)S(1)}, bf16[2,768,1024]{2,1,0:T(8,128)(2,1)S...) custom-call(bf16[40,1024]{1,0:T(8,128)(2,1)} %tok_h.1, bf16[40,1024]{1,0:T(8,128)(2,1)} %grad_h.1, ...), custom_call_target="tpu_custom_call" | custom-call | tf_op jit(solution)/shard_map/pallas_call | solution.py:524
  64.4 3.8 %shard_map.119 = (bf16[40,1024]{1,0:T(8,128)(2,1)}, bf16[40,1024]{1,0:T(8,128)(2,1)}, f32[8,40]{1,0:T(8,128)}, bf16[2,768,1024]{2,1,0:T(8,128)(2,1)}, bf16[2,768...) custom-call(bf16[40,1024]{1,0:T(8,128)(2,1)S(1)} %get-tuple-element.18.refs_0_, ...), custom_call_target="tpu_custom_call" | custom-call | tf_op jit(solution)/shard_map/pallas_call | solution.py:555

commit v3 on v2

v3 whole, which is shorter than its diff:
```python
import functools
import jax
import jax.numpy as jnp
from jax import lax
from jax.experimental import pallas as pl
from jax.experimental.pallas import tpu as pltpu
from jax.sharding import PartitionSpec as P

CAP = 240
F32 = jnp.float32
BF = jnp.bfloat16
VM = pl.BlockSpec(memory_space=pltpu.VMEM)
ANY = pl.BlockSpec(memory_space=pl.ANY)
HBM = pl.BlockSpec(memory_space=pltpu.HBM)
MESH = pl.DeviceIdType.MESH


def up_to(x, k):
    return (x + k - 1) // k * k


def factor(n):
    slow = 4 if n % 4 == 0 else 1
    return slow, n // slow


def flip(a, j):
    bit = 1
    while bit <= j:
        if j & bit:
            a = a + bit - 2 * bit * lax.rem(a // bit, 2)
        bit *= 2
    return a


def remote(src, dst, send, recv, where):
    return pltpu.make_async_remote_copy(
        src_ref=src, dst_ref=dst, send_sem=send, recv_sem=recv,
        device_id=where, device_id_type=MESH,
    )


def dotted(x, y, dx, dy):
    return lax.dot_general(x, y, (((dx,), (dy,)), ((), ())), preferred_element_type=F32)


class Plan:
    def __init__(self, n, nd, tb, top, e, f, d):
        self.n, self.nd, self.tb, self.top, self.e, self.f, self.d = n, nd, tb, top, e, f, d
        self.slow, self.fast = factor(n)
        self.m = nd // 2
        self.h = e // 2
        self.experts = n * e
        self.tbp = up_to(tb, 16)
        self.tl = up_to(n * self.tbp, 128)
        order = list(range(self.slow))
        self.zorder = order[0::2] + order[1::2]
        self.nz = max(1, self.slow // 2)
        self.early = self.zorder[:self.nz]
        self.late = self.zorder[self.nz:]
        self.hb = self.nz * self.fast * self.tbp
        n1 = self.nz * self.fast * tb
        n2 = n * tb - n1
        lo = max(0, CAP - n2) // 16 * 16
        hi = min(CAP, up_to(n1, 16))
        self.hi = hi
        spans = []
        half = up_to(self.hb, 128)
        back = self.hb // 128 * 128
        for s0, s1, l0, l1, needs_late in ((0, lo, 0, half, False), (lo, hi, 0, self.tl, True),
                                           (hi, CAP, back, self.tl, True)):
            if s1 > s0:
                spans.append((s0, s1, l0, l1, needs_late))
        self.spans = spans
        self.lo = lo
        self.half, self.back = half, back
        self.gs = (2 if d % 256 == 0 else 1, 1)
        self.q = 2 if d % 512 == 0 else 1
        self.qw = d // self.q
        self.first = [c for c in range(len(spans)) if not spans[c][4]]
        self.rest = [c for c in range(len(spans)) if spans[c][4]]
        self.slots = {}
        self.number()

    def number(self):
        nc, slow, fast, m = len(self.spans), self.slow, self.fast, self.m
        keys = [("load", i) for i in range(3)] + [("route", i) for i in range(2)]
        keys += [(k,) for k in ("meta send", "meta", "pair send", "cross send", "dots send", "dots")]
        for i in range(2):
            keys += [("own", i, g) for g in range(self.gs[i])] + [("z send", i), ("y send", i), ("share send", i)]
            for g in range(self.gs[i]):
                keys += [("z", i, jz, g) for jz in range(1, slow)]
                keys += [("y", i, jz, jj, g) for jz in range(slow) for jj in range(1, fast)]
            keys += [("share", i, c) for c in range(nc)]
        keys += [("pair", k, cs[0]) for k in (0, 1) for cs in (self.first, self.rest) if cs] + [("pair", 2, 0)]
        keys += [("cross", k, c, j) for k in range(3) for c in range(nc) for j in range(1, m)]
        for i in range(3):
            keys += [("ry send", i), ("rz send", i)]
            for q in range(self.q if i < 2 else 1):
                keys += [("ry", i, q, jz, jj) for jz in range(slow) for jj in range(1, fast)]
                keys += [("rz", i, q, jz) for jz in range(1, slow)]
        for key in keys:
            self.slots[key] = len(self.slots)

    def place(self, jz, jj):
        return self.zorder.index(jz) * self.fast + jj


def main_kernel(p, tok_h, grad_h, ids_h, wts_h, gw_h, uw_h, dw_h,
                layer_o, tgrad_o, rg_o, gate_o, up_o, down_o,
                ids, wts, hid, gud, rows, sgrad, gw, uw, dw, tokb, gradb, tokf, gradf, wown, wall, one, scaled, grows,
                psend, precv, mine, got, eb, terms, dmat, osend, isend, dsend,
                orb, irb, drb, oacc, iacc, dacc, ozb, izb, dzb, dots, sems):
    n, nd, tb, e, f, d = p.n, p.nd, p.tb, p.e, p.f, p.d
    slow, fast, m, h, tbp = p.slow, p.fast, p.m, p.h, p.tbp
    me = lax.axis_index("expert")
    dp = lax.axis_index("dp")
    a, b = me // fast, lax.rem(me, fast)
    chip, core = dp // 2, lax.rem(dp, 2)
    partner = {"dp": chip * 2 + 1 - core}
    spans = p.spans
    nc = len(spans)

    def at(*key):
        return sems.at[p.slots[key]]

    def drain(ref, *key):
        pltpu.make_async_copy(ref, ref, at(*key)).wait()

    gs, nq, qw = p.gs, p.q, p.qw

    def cols(i, g):
        return slice(g * (d // gs[i]), (g + 1) * (d // gs[i]))

    def strip(i, g):
        return (tok_h, grad_h)[i].at[:, cols(i, g)]

    sem = pltpu.get_barrier_semaphore()
    for j in range(1, n):
        pl.semaphore_signal(sem, inc=1, device_id={"expert": lax.rem(me + j, n)}, device_id_type=MESH)
    for j in range(1, nd):
        pl.semaphore_signal(sem, inc=1, device_id={"dp": lax.rem(dp + j, nd)}, device_id_type=MESH)
    loads = [pltpu.make_async_copy(x, y, at("load", i)) for i, (x, y) in enumerate(((gw_h, gw), (uw_h, uw), (dw_h, dw)))]
    mine_in = [[pltpu.make_async_copy(strip(i, g), y.at[me, g], at("own", i, g)) for g in range(gs[i])]
               for i, y in enumerate((tokb, gradb))]
    routing = [pltpu.make_async_copy(x, y, at("route", i)) for i, (x, y) in enumerate(((ids_h, ids), (wts_h, wts)))]
    for c in routing + mine_in[0] + loads[:2] + mine_in[1] + loads[2:]:
        c.start()
    pl.semaphore_wait(sem, n - 1 + nd - 1)

    blocks = (tokb, gradb)

    def source(jz, jj):
        return flip(a, jz) * fast + lax.rem(b - jj + fast, fast)

    def meta(j):
        return remote(wown, wall.at[me], at("meta send"), at("meta"), {"expert": lax.rem(me + j, n)})

    def zcopy(i, jz, g):
        return remote(strip(i, g), blocks[i].at[me, g], at("z send", i), at("z", i, jz, g),
                      {"expert": flip(a, jz) * fast + b})

    def ycopy(i, jz, jj, g):
        blk = source(jz, 0)
        src = strip(i, g) if jz == 0 else blocks[i].at[blk, g]
        return remote(src, blocks[i].at[blk, g], at("y send", i), at("y", i, jz, jj, g),
                      {"expert": a * fast + lax.rem(b + jj, fast)})

    def outward(i, jz):
        for g in range(gs[i]):
            zcopy(i, jz, g).start()

    def forward(i, jz):
        for g in range(gs[i]):
            if jz:
                zcopy(i, jz, g).wait_recv()
            for jj in range(1, fast):
                ycopy(i, jz, jj, g).start()

    def settle(i, group, flat):
        for jz in group:
            for jj in range(fast):
                row = p.place(jz, jj) * tbp
                for g in range(gs[i]):
                    if jj:
                        ycopy(i, jz, jj, g).wait_recv()
                    elif jz == 0:
                        mine_in[i][g].wait()
                    flat[row:row + tb, cols(i, g)] = blocks[i][source(jz, jj), g]

    head = [jz for jz in p.early + p.late if jz]
    for jz in head[:1]:
        outward(0, jz)
    forward(0, 0)

    for c in routing:
        c.wait()
    which = lax.broadcasted_iota(jnp.int32, (p.experts, tb), 0)
    w = jnp.zeros((p.experts, tb), F32)
    for k in range(p.top):
        w = w + jnp.where(which == ids[k:k + 1, :], wts[k:k + 1, :].astype(F32), 0.0)
    wown[...] = jnp.zeros_like(wown)
    wown[:, 0:tb] = w.astype(BF)
    wall[me] = wown[...]
    for j in range(1, n):
        meta(j).start()
    for jz in head[1:]:
        outward(0, jz)
    for jz in p.late[:1] + [jz for jz in head if jz not in p.late[:1]]:
        outward(1, jz)

    tokf[...] = jnp.zeros_like(tokf)
    gradf[...] = jnp.zeros_like(gradf)
    tl = p.tl
    lower = ((lax.broadcasted_iota(jnp.int32, (tl, tl), 0) < lax.broadcasted_iota(jnp.int32, (tl, tl), 1))
             & ((lax.broadcasted_iota(jnp.int32, (tl, tl), 0) < p.hb)
                == (lax.broadcasted_iota(jnp.int32, (tl, tl), 1) < p.hb)))
    lower = jnp.where(lower, 1.0, 0.0).astype(BF)

    tail = p.late[1:]
    for jz in p.early:
        if jz:
            forward(0, jz)
    for jz in p.late[:1]:
        forward(0, jz)
    forward(1, 0)
    drain(wall.at[0:n - 1], "meta")

    sub = lax.broadcasted_iota(jnp.int32, (p.experts, 128), 0)
    row = lax.broadcasted_iota(jnp.int32, (16, 128), 0)
    wl = jnp.zeros((16, tl), F32)
    for jz in p.zorder:
        for jj in range(fast):
            full = wall[source(jz, jj)].astype(F32)
            v = jnp.zeros((16, 128), F32)
            for i in range(e):
                v = jnp.where(row == i, jnp.sum(jnp.where(sub == me * e + i, full, 0.0), axis=0, keepdims=True), v)
            if tl > 128:
                v = jnp.concatenate([v, jnp.zeros((16, tl - 128), F32)], axis=1)
            to = p.place(jz, jj) * tbp
            wl = wl + (pltpu.roll(v, to, 1) if to else v)
    match = wl > 0.0
    rank = dotted(jnp.where(match, 1.0, 0.0).astype(BF), lower, 1, 0)
    lane = lax.broadcasted_iota(jnp.int32, (16, tl), 1)
    at_slot = jnp.where(match, jnp.where(lane < p.hb, rank, CAP - 1.0 - rank), -1.0)
    line = lax.broadcasted_iota(jnp.int32, (CAP, tl), 0).astype(F32)
    for i in range(e):
        pick = jnp.abs(line - at_slot[i:i + 1, :]) < 0.5
        one[i] = jnp.where(pick, 1.0, 0.0).astype(BF)
        scaled[i] = jnp.where(pick, wl[i:i + 1, :], 0.0).astype(BF)

    settle(0, p.early, tokf)

    def reach(cs):
        return spans[cs[0]][0], spans[cs[-1]][1]

    def take(table, flat, out, cs):
        for c in cs:
            s0, s1, l0, l1, _ = spans[c]
            for i in range(e):
                out[i, s0:s1] = dotted(table[i, s0:s1, l0:l1], flat[l0:l1], 1, 0).astype(BF)

    def product(k, i, cs):
        s0, s1 = reach(cs)
        left = (rows, rows, sgrad)[k]
        right = (gw, uw, dw)[k]
        return dotted(left[i, s0:s1], right[i], 1, 1)

    def pair(k, cs):
        s0, s1 = reach(cs)
        return remote(psend.at[k, :, s0:s1], precv.at[k, :, s0:s1], at("pair send"), at("pair", k, cs[0]), partner)

    def cross(k, c, j):
        s0, s1 = spans[c][:2]
        return remote(mine.at[k, :, s0:s1], got.at[k, j, :, s0:s1], at("cross send"), at("cross", k, c, j),
                      {"dp": lax.rem(chip + j, m) * 2 + core})

    def theirs(k, cs):
        s0, s1 = reach(cs)
        for u in range(h):
            psend[k, u, s0:s1] = product(k, (1 - core) * h + u, cs).astype(BF)
        pair(k, cs).start()

    def exchange(k, c):
        for j in range(1, m):
            cross(k, c, j).start()

    def ours(k, cs):
        g0 = spans[cs[0]][0]
        part = [product(k, core * h + u, cs) for u in range(h)]
        pair(k, cs).wait_recv()
        for c in cs:
            s0, s1 = spans[c][:2]
            for u in range(h):
                mine[k, u, s0:s1] = (part[u][s0 - g0:s1 - g0] + precv[k, u, s0:s1].astype(F32)).astype(BF)
            if k == 2 or c == cs[0]:
                exchange(k, c)

    def total(k, c, u):
        s0, s1 = spans[c][:2]
        v = mine[k, u, s0:s1].astype(F32)
        for j in range(1, m):
            v = v + got[k, j, u, s0:s1].astype(F32)
        return v

    def share(k, c):
        s0, s1 = spans[c][:2]
        mid = pl.ds(core * h, h)
        view = hid.at[mid, s0:s1] if k == 0 else gud.at[:, mid, s0:s1]
        return remote(view, view, at("share send", k), at("share", k, c), partner)

    def make_hidden(c):
        s0, s1 = spans[c][:2]
        for k in (0, 1):
            for j in range(1, m):
                cross(k, c, j).wait_recv()
        for u in range(h):
            gate, up = total(0, c, u), total(1, c, u)
            hid[core * h + u, s0:s1] = (gate * jax.nn.sigmoid(gate) * up).astype(BF)
        share(0, c).start()

    def make_delta(c):
        s0, s1 = spans[c][:2]
        for j in range(1, m):
            cross(2, c, j).wait_recv()
        for u in range(h):
            gate, up, hg = total(0, c, u), total(1, c, u), total(2, c, u)
            sig = jax.nn.sigmoid(gate)
            gud[0, core * h + u, s0:s1] = (hg * up * sig * (1.0 + gate * (1.0 - sig))).astype(BF)
            gud[1, core * h + u, s0:s1] = (hg * gate * sig).astype(BF)
        share(1, c).start()

    def back(table, i, s0, s1, l0, l1, x):
        return dotted(table[i, s0:s1, l0:l1], x, 0, 0)

    sends = (osend, isend, dsend)
    rbufs = (orb, irb, drb)
    accs = (oacc, iacc, dacc)
    zbufs = (ozb, izb, dzb)
    pieces = (nq, nq, 1)

    def ry(i, q, jz, jj):
        to = a * fast + lax.rem(b + jj, fast)
        return remote(sends[i].at[q, flip(a, jz) * fast + lax.rem(b + jj, fast)], rbufs[i].at[q, jz, jj],
                      at("ry send", i), at("ry", i, q, jz, jj), {"expert": to})

    def rz(i, q, jz):
        return remote(accs[i].at[q, jz], zbufs[i].at[q, jz], at("rz send", i), at("rz", i, q, jz),
                      {"expert": flip(a, jz) * fast + b})

    def reply(jz, jj):
        return flip(a, jz) * fast + lax.rem(b + jj, fast)

    def lanes_of(group):
        if group is p.early:
            return 0, p.half, 0
        return p.back, p.tl, p.hb - p.back

    fb = 256 if f % 256 == 0 else f

    def slots_of(group):
        return (0, p.hi) if group is p.early else (p.lo, CAP)

    def off(i, q, group):
        for jz in reversed(group):
            for jj in range(1, fast):
                ry(i, q, jz, jj).start()

    def send_piece(i, q, table, data, group):
        s0, s1 = slots_of(group)
        l0, l1, skip = lanes_of(group)
        v = sum(back(table, x, s0, s1, l0, l1, data[x, s0:s1, q * qw:(q + 1) * qw]) for x in range(e))
        for g, jz in enumerate(group):
            for jj in range(fast):
                row = skip + (g * fast + jj) * tbp
                sends[i][q, reply(jz, (fast - jj) % fast)] = v[row:row + tb].astype(BF)
        off(i, q, group)

    def out_part(cs, group):
        if cs:
            s0, s1 = reach(cs)
            dot = [jnp.zeros((s1 - s0, 1), F32) for _ in range(e)]
        for q in range(nq):
            c0, c1 = q * qw, (q + 1) * qw
            if cs:
                for i in range(e):
                    v = dotted(hid[i, s0:s1], dw[i, :, c0:c1], 1, 0)
                    eb[i, s0:s1, c0:c1] = v.astype(BF)
                    dot[i] = dot[i] + jnp.sum(v * grows[i, s0:s1, c0:c1].astype(F32), axis=1, keepdims=True)
            if group:
                send_piece(0, q, scaled, eb, group)
        if cs:
            for i in range(e):
                own = lax.broadcasted_iota(jnp.int32, (s1 - s0, dmat.shape[2]), 1) == me * e + i
                dmat[i, s0:s1] = jnp.where(own, dot[i], 0.0).astype(BF)
        if group:
            s0, s1 = slots_of(group)
            l0, l1, skip = lanes_of(group)
            v = sum(dotted(dmat[x, s0:s1], one[x, s0:s1, l0:l1], 0, 0) for x in range(e))[:p.experts]
            width = l1 - l0
            for g, jz in enumerate(group):
                for jj in range(fast):
                    row = skip + (g * fast + jj) * tbp
                    w = (pltpu.roll(v, (width - row) % width, 1) if row else v)[:, :128]
                    sends[2][0, reply(jz, (fast - jj) % fast)] = w.astype(BF)
            off(2, 0, group)

    def in_part(cs, group, q):
        c0, c1 = q * qw, (q + 1) * qw
        if cs:
            s0, s1 = reach(cs)
            for i in range(e):
                terms[i, s0:s1, c0:c1] = (dotted(gud[0, i, s0:s1], gw[i, :, c0:c1], 1, 0)
                                          + dotted(gud[1, i, s0:s1], uw[i, :, c0:c1], 1, 0)).astype(BF)
        if group:
            send_piece(1, q, one, terms, group)

    def pass_on(i, q, group):
        for jz in reversed(group):
            v = sends[i][q, flip(a, jz) * fast + b].astype(F32)
            for jj in range(1, fast):
                ry(i, q, jz, jj).wait_recv()
                v = v + rbufs[i][q, jz, jj].astype(F32)
            accs[i][q, jz] = v.astype(BF)
            if jz:
                rz(i, q, jz).start()

    def result(i, q):
        v = accs[i][q, 0].astype(F32)
        for jz in range(1, slow):
            rz(i, q, jz).wait_recv()
            v = v + zbufs[i][q, jz].astype(F32)
        return v

    def share_recv(k, cs):
        for c in cs:
            share(k, c).wait_recv()

    def weight_grad(out, left, right, i):
        for c0 in range(0, f, fb):
            out[i, c0:c0 + fb] = dotted(left[i, :, c0:c0 + fb], right[i], 0, 0).astype(BF)

    first, rest = p.first, p.rest
    every = list(range(nc))
    near = [c for c in every if spans[c][0] < p.hi]
    far = [c for c in every if spans[c][0] >= p.hi]
    done = [c for c in first if c in near]

    loads[0].wait()
    if first:
        take(one, tokf, rows, first)
        theirs(0, first)
        ours(0, first)
    for jz in tail:
        forward(0, jz)
    for jz in p.late[:1]:
        forward(1, jz)
    loads[1].wait()
    if first:
        theirs(1, first)
        ours(1, first)
    settle(0, p.late, tokf)
    for jz in p.early:
        if jz:
            forward(1, jz)
    if rest:
        take(one, tokf, rows, rest)
        theirs(0, rest)
    for jz in tail:
        forward(1, jz)
    if rest:
        ours(0, rest)
        theirs(1, rest)
        ours(1, rest)
        for c in rest[1:]:
            for k in (0, 1):
                exchange(k, c)
    for c in done:
        make_hidden(c)
    loads[2].wait()
    settle(1, p.zorder, gradf)
    take(scaled, gradf, sgrad, every)
    theirs(2, every)
    take(one, gradf, grows, every)
    ours(2, every)
    for c in near:
        if c not in done:
            make_hidden(c)
    share_recv(0, near)
    out_part(near, p.early)
    for c in far:
        make_hidden(c)
    pass_on(2, 0, p.early)
    for q in range(nq):
        pass_on(0, q, p.early)
    share_recv(0, far)
    out_part(far, p.late)
    for c in near[:1]:
        make_delta(c)
    weight_grad(down_o, hid, sgrad, 0)
    for c in near[1:]:
        make_delta(c)
    for i in range(1, e):
        weight_grad(down_o, hid, sgrad, i)
    share_recv(1, near)
    for q in range(nq):
        in_part(near, p.early, q)
    for c in far:
        make_delta(c)
    pass_on(2, 0, p.late)
    for q in range(nq):
        pass_on(0, q, p.late)
    share_recv(1, far)
    for q in range(nq):
        in_part(far, p.late, q)
        pass_on(1, q, p.early)
    jobs = [(gate_o, gud.at[0], rows, i) for i in range(e)] + [(up_o, gud.at[1], rows, i) for i in range(e)]

    def job():
        if jobs:
            weight_grad(*jobs.pop(0))

    def across(j):
        return remote(dots.at[0], dots.at[j], at("dots send"), at("dots"), {"dp": lax.rem(dp + j, nd)})

    dots[0] = result(2, 0).astype(BF)
    for j in range(1, nd):
        across(j).start()
    job()
    for q in range(nq):
        pass_on(1, q, p.late)
        if q < nq - 1:
            job()
    while jobs:
        job()
    drain(dots.at[0:nd - 1], "dots")
    v = dots[0].astype(F32)
    for j in range(1, nd):
        v = v + dots[j].astype(F32)
    v = v[:, :tb]
    for k in range(p.top):
        rg_o[k:k + 1, :] = jnp.sum(jnp.where(which == ids[k:k + 1, :], v, 0.0), axis=0, keepdims=True)
    for i, out in ((0, layer_o), (1, tgrad_o)):
        for q in range(nq):
            out[:, q * qw:(q + 1) * qw] = result(i, q).astype(BF)

    drain(wall.at[0:n - 1], "meta send")
    drain(dots.at[0:nd - 1], "dots send")
    for i in range(2):
        if slow > 1:
            drain(blocks[i].at[0:slow - 1], "z send", i)
        if fast > 1:
            drain(blocks[i].at[0:slow * (fast - 1)], "y send", i)
    drain(psend, "pair send")
    if m > 1:
        drain(got.at[:, 1:m], "cross send")
    drain(hid.at[0:h], "share send", 0)
    drain(gud.at[:, 0:h], "share send", 1)
    for i in range(3):
        if slow > 1:
            drain(accs[i].at[:, 0:slow - 1], "rz send", i)
        if fast > 1:
            drain(sends[i].at[:, 0:slow * (fast - 1)], "ry send", i)


def main_call(n, nd, tok, grad, ids, wts, gw, uw, dw):
    e, f, d = gw.shape
    tb, top = tok.shape[0], ids.shape[0]
    p = Plan(n, nd, tb, top, e, f, d)
    nc = len(p.spans)
    vm, dma = pltpu.VMEM, pltpu.SemaphoreType.DMA
    piece, el = (tb, p.qw), up_to(p.experts, 128)
    dot = (p.experts, 128)
    per_half = (p.h, CAP, f)
    return pl.pallas_call(
        functools.partial(main_kernel, p),
        out_shape=[vm((tb, d), BF), vm((tb, d), BF), vm((top, tb), F32)] + [vm((e, f, d), BF)] * 3,
        in_specs=[HBM] * 7,
        out_specs=[VM] * 6,
        scratch_shapes=[vm((top, tb), jnp.int32), vm((top, tb), BF)] + [vm((e, CAP, f), BF), vm((2, e, CAP, f), BF)] + [vm((e, CAP, d), BF)] * 2 + [vm((e, f, d), BF)] * 3 + [vm((n, g, tb, d // g), BF) for g in p.gs] + [vm((p.tl, d), BF)] * 2
        + [vm(dot, BF), vm((n,) + dot, BF)] + [vm((e, CAP, p.tl), BF)] * 2 + [vm((e, CAP, d), BF)]
        + [vm((3,) + per_half, BF)] * 3 + [vm((3, p.m) + per_half, BF)]
        + [vm((e, CAP, d), BF)] * 2 + [vm((e, CAP, el), BF)]
        + [vm((p.q, n) + piece, BF)] * 2 + [vm((1, n) + dot, BF)]
        + [vm((p.q, p.slow, p.fast) + piece, BF)] * 2 + [vm((1, p.slow, p.fast) + dot, BF)]
        + ([vm((p.q, p.slow) + piece, BF)] * 2 + [vm((1, p.slow) + dot, BF)]) * 2
        + [vm((nd,) + dot, BF)]
        + [dma((len(p.slots),))],
        compiler_params=pltpu.CompilerParams(collective_id=0, has_side_effects=True, vmem_limit_bytes=44 << 20),
    )(*[pltpu.with_memory_space_constraint(x, pltpu.HBM) for x in (tok, grad, ids, wts, gw, uw, dw)])


def flush_kernel(k, *refs):
    ins, outs, sem = refs[:k], refs[k:2 * k], refs[2 * k]
    copies = [pltpu.make_async_copy(x, y, sem.at[i]) for i, (x, y) in enumerate(zip(ins, outs))]
    for c in copies:
        c.start()
    for c in copies:
        c.wait()


def flush(*arrays):
    k = len(arrays)
    return pl.pallas_call(
        functools.partial(flush_kernel, k),
        out_shape=[jax.ShapeDtypeStruct(x.shape, x.dtype) for x in arrays],
        in_specs=[VM] * k, out_specs=[ANY] * k,
        scratch_shapes=[pltpu.SemaphoreType.DMA((k,))],
        compiler_params=pltpu.CompilerParams(vmem_limit_bytes=4 << 20),
    )(*[pltpu.with_memory_space_constraint(x, pltpu.VMEM) for x in arrays])


def body(n, nd, tokens, expert_ids, routing_weights, gate_weight, up_weight, down_weight, out_grad):
    layer, tgrad, rg, gate_grad, up_grad, down_grad = flush(*main_call(
        n, nd, tokens, out_grad, expert_ids.T, routing_weights.T, gate_weight, up_weight, down_weight))
    return layer, tgrad, rg.T, gate_grad, up_grad, down_grad


def solution(mesh):
    n, nd = mesh.shape["expert"], mesh.shape["dp"]
    w = P("expert", None, "dp")
    x = P("expert", "dp")
    r = P("expert", None)
    return jax.shard_map(functools.partial(body, n, nd), mesh=mesh, in_specs=(x, r, r, w, w, w, x),
                         out_specs=(x, x, r, w, w, w), check_vma=False)
```

time: 68.6 us -> 65.3 us (0.952)
  Pallas kernels: 67.6 us -> 64.3 us
    pallas_call x1, Pallas kernels: 63.7 us -> 60.5 us  [main_call(): pl.pallas_call(functools.partial(main_kernel, p), out_shape=[vm((tb, d),...]
where the time goes in v3:
time: 65.3 us; the launch traced here: 65.1 us
  Pallas kernels  64.3 us (98%)
  between operations  0.8 us (1%)
    pallas_call x1, Pallas kernels, main_call(): pl.pallas_call(functools.partial(main_kernel, p), out_shape=[vm((tb, d),...  60.5 us
    pallas_call x1, Pallas kernels, flush(): pl.pallas_call(functools.partial(flush_kernel, k), out_shape=[jax.ShapeDt...  3.85 us

profile of v3, /device:TPU:0, one launch (start us, length us, event | category | flops | bytes accessed | tf_op | source)
XLA Modules:
  0.0 65.1 jit_solution(15079703069103429923)
XLA Ops:
  0.6 60.5 %shard_map.118 = (bf16[40,1024]{1,0:T(8,128)(2,1)S(1)}, bf16[40,1024]{1,0:T(8,128)(2,1)S(1)}, f32[8,40]{1,0:T(8,128)S(1)}, bf16[2,768,1024]{2,1,0:T(8,128)(2,1)S...) custom-call(bf16[40,1024]{1,0:T(8,128)(2,1)} %tok_h.1, bf16[40,1024]{1,0:T(8,128)(2,1)} %grad_h.1, ...), custom_call_target="tpu_custom_call" | custom-call | tf_op jit(solution)/shard_map/pallas_call | solution.py:575
  61.1 3.8 %shard_map.119 = (bf16[40,1024]{1,0:T(8,128)(2,1)}, bf16[40,1024]{1,0:T(8,128)(2,1)}, f32[8,40]{1,0:T(8,128)}, bf16[2,768,1024]{2,1,0:T(8,128)(2,1)}, bf16[2,768...) custom-call(bf16[40,1024]{1,0:T(8,128)(2,1)S(1)} %get-tuple-element.18.refs_0_, ...), custom_call_target="tpu_custom_call" | custom-call | tf_op jit(solution)/shard_map/pallas_call | solution.py:604

commit v4 on v3

--- a/solution.py
+++ b/solution.py
@@ -166,12 +166,12 @@
         return remote(src, blocks[i].at[blk, g], at("y send", i), at("y", i, jz, jj, g),
                       {"expert": a * fast + lax.rem(b + jj, fast)})
 
-    def outward(i, jz):
-        for g in range(gs[i]):
+    def outward(i, jz, some=None):
+        for g in range(gs[i]) if some is None else some:
             zcopy(i, jz, g).start()
 
-    def forward(i, jz):
-        for g in range(gs[i]):
+    def forward(i, jz, some=None):
+        for g in range(gs[i]) if some is None else some:
             if jz:
                 zcopy(i, jz, g).wait_recv()
             for jj in range(1, fast):
@@ -189,9 +189,6 @@
                     flat[row:row + tb, cols(i, g)] = blocks[i][source(jz, jj), g]
 
     head = [jz for jz in p.early + p.late if jz]
-    for jz in head[:1]:
-        outward(0, jz)
-    forward(0, 0)
 
     for c in routing:
         c.wait()
@@ -204,6 +201,9 @@
     wall[me] = wown[...]
     for j in range(1, n):
         meta(j).start()
+    for jz in head[:1]:
+        outward(0, jz)
+    forward(0, 0)
     for jz in head[1:]:
         outward(0, jz)
     for jz in p.late[:1] + [jz for jz in head if jz not in p.late[:1]]:
@@ -218,38 +218,43 @@
     lower = jnp.where(lower, 1.0, 0.0).astype(BF)
 
     tail = p.late[1:]
-    for jz in p.early:
-        if jz:
-            forward(0, jz)
-    for jz in p.late[:1]:
-        forward(0, jz)
-    forward(1, 0)
-    drain(wall.at[0:n - 1], "meta")
-
+
+    def routed():
+        drain(wall.at[0:n - 1], "meta")
+
+    routed()
     sub = lax.broadcasted_iota(jnp.int32, (p.experts, 128), 0)
-    row = lax.broadcasted_iota(jnp.int32, (16, 128), 0)
-    wl = jnp.zeros((16, tl), F32)
+    er = up_to(e, 8)
+    row = lax.broadcasted_iota(jnp.int32, (er, 128), 0)
+    wl = jnp.zeros((er, tl), F32)
     for jz in p.zorder:
         for jj in range(fast):
             full = wall[source(jz, jj)].astype(F32)
-            v = jnp.zeros((16, 128), F32)
+            v = jnp.zeros((er, 128), F32)
             for i in range(e):
                 v = jnp.where(row == i, jnp.sum(jnp.where(sub == me * e + i, full, 0.0), axis=0, keepdims=True), v)
             if tl > 128:
-                v = jnp.concatenate([v, jnp.zeros((16, tl - 128), F32)], axis=1)
+                v = jnp.concatenate([v, jnp.zeros((er, tl - 128), F32)], axis=1)
             to = p.place(jz, jj) * tbp
             wl = wl + (pltpu.roll(v, to, 1) if to else v)
     match = wl > 0.0
     rank = dotted(jnp.where(match, 1.0, 0.0).astype(BF), lower, 1, 0)
-    lane = lax.broadcasted_iota(jnp.int32, (16, tl), 1)
+    lane = lax.broadcasted_iota(jnp.int32, (er, tl), 1)
     at_slot = jnp.where(match, jnp.where(lane < p.hb, rank, CAP - 1.0 - rank), -1.0)
+    settle(0, p.early[:1], tokf)
+    for jz in p.early[1:]:
+        forward(0, jz, [0])
     line = lax.broadcasted_iota(jnp.int32, (CAP, tl), 0).astype(F32)
     for i in range(e):
         pick = jnp.abs(line - at_slot[i:i + 1, :]) < 0.5
         one[i] = jnp.where(pick, 1.0, 0.0).astype(BF)
-        scaled[i] = jnp.where(pick, wl[i:i + 1, :], 0.0).astype(BF)
-
-    settle(0, p.early, tokf)
+
+    for jz in p.early[1:]:
+        forward(0, jz, range(1, gs[0]))
+    for jz in p.late[:1]:
+        forward(0, jz)
+    forward(1, 0)
+    settle(0, p.early[1:], tokf)
 
     def reach(cs):
         return spans[cs[0]][0], spans[cs[-1]][1]
@@ -357,6 +362,7 @@
         return p.back, p.tl, p.hb - p.back
 
     fb = 256 if f % 256 == 0 else f
+    fd = 256 if d % 256 == 0 else d
 
     def slots_of(group):
         return (0, p.hi) if group is p.early else (p.lo, CAP)
@@ -376,42 +382,60 @@
                 sends[i][q, reply(jz, (fast - jj) % fast)] = v[row:row + tb].astype(BF)
         off(i, q, group)
 
+    def share_recv(k, cs):
+        for c in cs:
+            share(k, c).wait_recv()
+
+    owned = [core * h + u for u in range(h)]
+    others = [(1 - core) * h + u for u in range(h)]
+
+    def out_rows(cs, which_ones):
+        s0, s1 = reach(cs)
+        for i in which_ones:
+            dot = jnp.zeros((s1 - s0, 1), F32)
+            for c0 in range(0, d, fd):
+                v = dotted(hid[i, s0:s1], dw[i, :, c0:c0 + fd], 1, 0)
+                eb[i, s0:s1, c0:c0 + fd] = v.astype(BF)
+                dot = dot + jnp.sum(v * grows[i, s0:s1, c0:c0 + fd].astype(F32), axis=1, keepdims=True)
+            own = lax.broadcasted_iota(jnp.int32, (s1 - s0, dmat.shape[2]), 1) == me * e + i
+            dmat[i, s0:s1] = jnp.where(own, dot, 0.0).astype(BF)
+
     def out_part(cs, group):
         if cs:
-            s0, s1 = reach(cs)
-            dot = [jnp.zeros((s1 - s0, 1), F32) for _ in range(e)]
+            out_rows(cs, owned)
+            share_recv(0, cs)
+            out_rows(cs, others)
+        if not group:
+            return
         for q in range(nq):
-            c0, c1 = q * qw, (q + 1) * qw
-            if cs:
-                for i in range(e):
-                    v = dotted(hid[i, s0:s1], dw[i, :, c0:c1], 1, 0)
-                    eb[i, s0:s1, c0:c1] = v.astype(BF)
-                    dot[i] = dot[i] + jnp.sum(v * grows[i, s0:s1, c0:c1].astype(F32), axis=1, keepdims=True)
-            if group:
-                send_piece(0, q, scaled, eb, group)
+            send_piece(0, q, scaled, eb, group)
+        s0, s1 = slots_of(group)
+        l0, l1, skip = lanes_of(group)
+        v = sum(dotted(dmat[x, s0:s1], one[x, s0:s1, l0:l1], 0, 0) for x in range(e))[:p.experts]
+        width = l1 - l0
+        for g, jz in enumerate(group):
+            for jj in range(fast):
+                row = skip + (g * fast + jj) * tbp
+                w = (pltpu.roll(v, (width - row) % width, 1) if row else v)[:, :128]
+                sends[2][0, reply(jz, (fast - jj) % fast)] = w.astype(BF)
+        off(2, 0, group)
+
+    def in_rows(cs, which_ones, q):
+        s0, s1 = reach(cs)
+        c0, c1 = q * qw, (q + 1) * qw
+        for i in which_ones:
+            terms[i, s0:s1, c0:c1] = (dotted(gud[0, i, s0:s1], gw[i, :, c0:c1], 1, 0)
+                                      + dotted(gud[1, i, s0:s1], uw[i, :, c0:c1], 1, 0)).astype(BF)
+
+    def in_first(cs):
         if cs:
-            for i in range(e):
-                own = lax.broadcasted_iota(jnp.int32, (s1 - s0, dmat.shape[2]), 1) == me * e + i
-                dmat[i, s0:s1] = jnp.where(own, dot[i], 0.0).astype(BF)
-        if group:
-            s0, s1 = slots_of(group)
-            l0, l1, skip = lanes_of(group)
-            v = sum(dotted(dmat[x, s0:s1], one[x, s0:s1, l0:l1], 0, 0) for x in range(e))[:p.experts]
-            width = l1 - l0
-            for g, jz in enumerate(group):
-                for jj in range(fast):
-                    row = skip + (g * fast + jj) * tbp
-                    w = (pltpu.roll(v, (width - row) % width, 1) if row else v)[:, :128]
-                    sends[2][0, reply(jz, (fast - jj) % fast)] = w.astype(BF)
-            off(2, 0, group)
+            for q in range(nq):
+                in_rows(cs, owned, q)
+            share_recv(1, cs)
 
     def in_part(cs, group, q):
-        c0, c1 = q * qw, (q + 1) * qw
         if cs:
-            s0, s1 = reach(cs)
-            for i in range(e):
-                terms[i, s0:s1, c0:c1] = (dotted(gud[0, i, s0:s1], gw[i, :, c0:c1], 1, 0)
-                                          + dotted(gud[1, i, s0:s1], uw[i, :, c0:c1], 1, 0)).astype(BF)
+            in_rows(cs, others, q)
         if group:
             send_piece(1, q, one, terms, group)
 
@@ -432,10 +456,6 @@
             v = v + zbufs[i][q, jz].astype(F32)
         return v
 
-    def share_recv(k, cs):
-        for c in cs:
-            share(k, c).wait_recv()
-
     def weight_grad(out, left, right, i):
         for c0 in range(0, f, fb):
             out[i, c0:c0 + fb] = dotted(left[i, :, c0:c0 + fb], right[i], 0, 0).astype(BF)
@@ -447,17 +467,20 @@
     done = [c for c in first if c in near]
 
     loads[0].wait()
+    loads[1].wait()
     if first:
         take(one, tokf, rows, first)
         theirs(0, first)
-        ours(0, first)
     for jz in tail:
         forward(0, jz)
+    if first:
+        ours(0, first)
+        theirs(1, first)
     for jz in p.late[:1]:
         forward(1, jz)
-    loads[1].wait()
+    for i in range(e):
+        scaled[i] = one[i] * wl[i:i + 1, :].astype(BF)
     if first:
-        theirs(1, first)
         ours(1, first)
     settle(0, p.late, tokf)
     for jz in p.early:
@@ -486,15 +509,13 @@
     for c in near:
         if c not in done:
             make_hidden(c)
-    share_recv(0, near)
     out_part(near, p.early)
     for c in far:
         make_hidden(c)
+    out_part(far, p.late)
     pass_on(2, 0, p.early)
     for q in range(nq):
         pass_on(0, q, p.early)
-    share_recv(0, far)
-    out_part(far, p.late)
     for c in near[:1]:
         make_delta(c)
     weight_grad(down_o, hid, sgrad, 0)
@@ -502,15 +523,14 @@
         make_delta(c)
     for i in range(1, e):
         weight_grad(down_o, hid, sgrad, i)
-    share_recv(1, near)
+    in_first(near)
     for q in range(nq):
         in_part(near, p.early, q)
+        pass_on(0, q, p.late)
     for c in far:
         make_delta(c)
     pass_on(2, 0, p.late)
-    for q in range(nq):
-        pass_on(0, q, p.late)
-    share_recv(1, far)
+    in_first(far)
     for q in range(nq):
         in_part(far, p.late, q)
         pass_on(1, q, p.early)
@@ -523,12 +543,13 @@
     def across(j):
         return remote(dots.at[0], dots.at[j], at("dots send"), at("dots"), {"dp": lax.rem(dp + j, nd)})
 
-    dots[0] = result(2, 0).astype(BF)
-    for j in range(1, nd):
-        across(j).start()
     job()
     for q in range(nq):
         pass_on(1, q, p.late)
+        if q == 0:
+            dots[0] = result(2, 0).astype(BF)
+            for j in range(1, nd):
+                across(j).start()
         if q < nq - 1:
             job()
     while jobs:
@@ -592,7 +613,15 @@
 
 def flush_kernel(k, *refs):
     ins, outs, sem = refs[:k], refs[k:2 * k], refs[2 * k]
-    copies = [pltpu.make_async_copy(x, y, sem.at[i]) for i, (x, y) in enumerate(zip(ins, outs))]
+    pairs = []
+    for x, y in zip(ins, outs):
+        if len(x.shape) == 3:
+            half = x.shape[1] // 2
+            for i in range(x.shape[0]):
+                pairs += [(x.at[i, r:r + half], y.at[i, r:r + half]) for r in (0, half)]
+        else:
+            pairs.append((x, y))
+    copies = [pltpu.make_async_copy(x, y, sem.at[i]) for i, (x, y) in enumerate(pairs)]
     for c in copies:
         c.start()
     for c in copies:
@@ -605,7 +634,7 @@
         functools.partial(flush_kernel, k),
         out_shape=[jax.ShapeDtypeStruct(x.shape, x.dtype) for x in arrays],
         in_specs=[VM] * k, out_specs=[ANY] * k,
-        scratch_shapes=[pltpu.SemaphoreType.DMA((k,))],
+        scratch_shapes=[pltpu.SemaphoreType.DMA((sum(2 * x.shape[0] if x.ndim == 3 else 1 for x in arrays),))],
         compiler_params=pltpu.CompilerParams(vmem_limit_bytes=4 << 20),
     )(*[pltpu.with_memory_space_constraint(x, pltpu.VMEM) for x in arrays])
 

time: 65.3 us -> 63.8 us (0.977)
  Pallas kernels: 64.3 us -> 62.9 us
    pallas_call x1, Pallas kernels: 60.5 us -> 59.1 us  [main_call(): pl.pallas_call(functools.partial(main_kernel, p), out_shape=[vm((tb, d),...]
where the time goes in v4:
time: 63.8 us; the launch traced here: 63.7 us
  Pallas kernels  62.9 us (99%)
  between operations  0.8 us (1%)
    pallas_call x1, Pallas kernels, main_call(): pl.pallas_call(functools.partial(main_kernel, p), out_shape=[vm((tb, d),...  59.1 us
    pallas_call x1, Pallas kernels, flush(): pl.pallas_call(functools.partial(flush_kernel, k), out_shape=[jax.ShapeDt...  3.81 us

profile of v4, /device:TPU:0, one launch (start us, length us, event | category | flops | bytes accessed | tf_op | source)
XLA Modules:
  0.0 63.7 jit_solution(11660001267932483025)
XLA Ops:
  0.6 59.1 %shard_map.118 = (bf16[40,1024]{1,0:T(8,128)(2,1)S(1)}, bf16[40,1024]{1,0:T(8,128)(2,1)S(1)}, f32[8,40]{1,0:T(8,128)S(1)}, bf16[2,768,1024]{2,1,0:T(8,128)(2,1)S...) custom-call(bf16[40,1024]{1,0:T(8,128)(2,1)} %tok_h.1, bf16[40,1024]{1,0:T(8,128)(2,1)} %grad_h.1, ...), custom_call_target="tpu_custom_call" | custom-call | tf_op jit(solution)/shard_map/pallas_call | solution.py:596
  59.7 3.8 %shard_map.119 = (bf16[40,1024]{1,0:T(8,128)(2,1)}, bf16[40,1024]{1,0:T(8,128)(2,1)}, f32[8,40]{1,0:T(8,128)}, bf16[2,768,1024]{2,1,0:T(8,128)(2,1)}, bf16[2,768...) custom-call(bf16[40,1024]{1,0:T(8,128)(2,1)S(1)} %get-tuple-element.18.refs_0_, ...), custom_call_target="tpu_custom_call" | custom-call | tf_op jit(solution)/shard_map/pallas_call | solution.py:633

commit v5 on v4

--- a/solution.py
+++ b/solution.py
@@ -144,7 +144,7 @@
     mine_in = [[pltpu.make_async_copy(strip(i, g), y.at[me, g], at("own", i, g)) for g in range(gs[i])]
                for i, y in enumerate((tokb, gradb))]
     routing = [pltpu.make_async_copy(x, y, at("route", i)) for i, (x, y) in enumerate(((ids_h, ids), (wts_h, wts)))]
-    for c in routing + mine_in[0] + loads[:2] + mine_in[1] + loads[2:]:
+    for c in routing:
         c.start()
     pl.semaphore_wait(sem, n - 1 + nd - 1)
 
@@ -208,6 +208,9 @@
         outward(0, jz)
     for jz in p.late[:1] + [jz for jz in head if jz not in p.late[:1]]:
         outward(1, jz)
+
+    for c in mine_in[0] + loads[:2] + mine_in[1] + loads[2:]:
+        c.start()
 
     tokf[...] = jnp.zeros_like(tokf)
     gradf[...] = jnp.zeros_like(gradf)

time: 63.8 us -> 63.8 us (level)
  no operation moved by 1% of the time
where the time goes in v5:
time: 63.8 us; the launch traced here: 63.7 us
  Pallas kernels  62.9 us (99%)
  between operations  0.8 us (1%)
    pallas_call x1, Pallas kernels, main_call(): pl.pallas_call(functools.partial(main_kernel, p), out_shape=[vm((tb, d),...  59.1 us
    pallas_call x1, Pallas kernels, flush(): pl.pallas_call(functools.partial(flush_kernel, k), out_shape=[jax.ShapeDt...  3.81 us

profile of v5, /device:TPU:0, one launch (start us, length us, event | category | flops | bytes accessed | tf_op | source)
XLA Modules:
  0.0 63.7 jit_solution(573793907750537724)
XLA Ops:
  0.6 59.1 %shard_map.118 = (bf16[40,1024]{1,0:T(8,128)(2,1)S(1)}, bf16[40,1024]{1,0:T(8,128)(2,1)S(1)}, f32[8,40]{1,0:T(8,128)S(1)}, bf16[2,768,1024]{2,1,0:T(8,128)(2,1)S...) custom-call(bf16[40,1024]{1,0:T(8,128)(2,1)} %tok_h.1, bf16[40,1024]{1,0:T(8,128)(2,1)} %grad_h.1, ...), custom_call_target="tpu_custom_call" | custom-call | tf_op jit(solution)/shard_map/pallas_call | solution.py:599
  59.7 3.8 %shard_map.119 = (bf16[40,1024]{1,0:T(8,128)(2,1)}, bf16[40,1024]{1,0:T(8,128)(2,1)}, f32[8,40]{1,0:T(8,128)}, bf16[2,768,1024]{2,1,0:T(8,128)(2,1)}, bf16[2,768...) custom-call(bf16[40,1024]{1,0:T(8,128)(2,1)S(1)} %get-tuple-element.18.refs_0_, ...), custom_call_target="tpu_custom_call" | custom-call | tf_op jit(solution)/shard_map/pallas_call | solution.py:636
